TPU v7x, 32 devices: a whole 2x2x4 slice. The times are simulated.
32 devices in a mesh: grp: 2 (over x), row: 8 (over z, y), col: 2 (over core).
Axes of the slice: x: 2, y: 2, z: 4, core: 2. Of those that a mesh axis runs over, the one named last changes fastest.
Arguments:
- query_window: bfloat16 [16, 8, 128, 1280], P(('grp', 'row'), 'col'), parts along dimension 0, may hold values from -80 to 80
- key_window: bfloat16 [16, 8, 128, 1280], P(('grp', 'row'), 'col'), parts along dimension 0, may hold values from -9 to 9
- value_window: bfloat16 [16, 8, 128, 1280], P(('grp', 'row'), 'col'), parts along dimension 0, may hold values from -6 to 6
- query_index: bfloat16 [16, 8, 128, 1280], P(('grp', 'row'), 'col'), parts along dimension 0, may hold values from -80 to 80
- key_index: bfloat16 [16, 8, 128, 1280], P(('grp', 'row'), 'col'), parts along dimension 0, may hold values from -9 to 9
- proj_weight: bfloat16 [1280, 1024], replicated, may hold values from -0.5 to 0.5
- proj_bias: float32 [1024], replicated, may hold values from -3 to 3
- first_kernel: bfloat16 [3, 3, 256, 256], replicated, may hold values from -0.125 to 0.125
- first_bias: float32 [256], replicated, may hold values from -3 to 3
- second_kernel: bfloat16 [3, 3, 256, 256], replicated, may hold values from -0.125 to 0.125
- second_bias: float32 [256], replicated, may hold values from -3 to 3
Outputs:
- fine_field: bfloat16 [256, 256, 256], P(('grp', 'row'), 'col'), parts along dimension 0
There are 2 independent parts, one for each index of `grp`. A program takes and returns all parts, laid end to end along the dimension named above; an argument that names none is the same for every part. Nothing has to cross between parts.
All inputs are finite; a program needn't handle non-finite values.
Results may differ from a plain program's by a relative error of at most 0.0048.
Values may be sent and summed in bfloat16 or wider, within the bound.
A program may use at most 64 MiB of HBM per device.

v0:
```python
import math

import jax
import jax.numpy as jnp
from jax import lax
from jax.sharding import PartitionSpec as P

HEADS = 8
HEAD_DIM = 160
CHANNELS = 256
TILE_ROWS = 8
TILE_COLS = 16


def extended(value, sides, width):
    for axis, dim in sides:
        size, length = (lax.axis_size(axis), value.shape[dim])
        up = [(i, (i + 1) % size) for i in range(size - 1)]
        down = [(j, i) for i, j in up]
        last = lax.slice_in_dim(value, length - width, length, axis=dim)
        first = lax.slice_in_dim(value, 0, width, axis=dim)
        before = lax.ppermute(last, axis, up)
        after = lax.ppermute(first, axis, down)
        value = jnp.concatenate([before, value, after], axis=dim)
    return value


def softmax_rows(scores):
    highest = jnp.max(scores, axis=-1, keepdims=True)
    raised = jnp.exp(scores - highest)
    return (raised / jnp.sum(raised, axis=-1, keepdims=True)).astype(jnp.bfloat16)


def window_attend(queries, key_rows, values):
    scores = jnp.einsum(
        "blhd,bmhd->bhlm", queries, key_rows, preferred_element_type=jnp.float32
    ) / math.sqrt(HEAD_DIM)
    weights = softmax_rows(scores)
    return jnp.einsum(
        "bhlm,bmhd->blhd", weights, values, preferred_element_type=jnp.float32
    ).astype(jnp.bfloat16)


def index_attend(queries, key_rows, values):
    scores = jnp.einsum(
        "lbhd,mbhd->bhlm", queries, key_rows, preferred_element_type=jnp.float32
    ) / math.sqrt(HEAD_DIM)
    weights = softmax_rows(scores)
    return jnp.einsum(
        "bhlm,mbhd->lbhd", weights, values, preferred_element_type=jnp.float32
    ).astype(jnp.bfloat16)


def convolve(image, kernel, bias):
    height, breadth, depth = image.shape
    padded = extended(image, (("row", 0), ("col", 1)), 1)
    total = jnp.zeros((height * breadth, kernel.shape[-1]), jnp.float32)
    for row_shift in range(3):
        for col_shift in range(3):
            cells = padded[row_shift : row_shift + height, col_shift : col_shift + breadth].reshape(
                -1, depth
            )
            total = total + jnp.dot(
                cells, kernel[row_shift, col_shift], preferred_element_type=jnp.float32
            )
    return (total + bias).reshape(height, breadth, -1)


def shards(
    query_window,
    key_window,
    value_window,
    query_index,
    key_index,
    proj_weight,
    proj_bias,
    first_kernel,
    first_bias,
    second_kernel,
    second_bias,
):
    rows_dev, cols_dev, tokens_win, features = query_window.shape
    layout = (rows_dev * cols_dev, tokens_win, HEADS, HEAD_DIM)
    window_out = window_attend(
        query_window.reshape(layout), key_window.reshape(layout), value_window.reshape(layout)
    ).reshape(query_window.shape)
    count_row = lax.axis_size("row")
    count_col = lax.axis_size("col")
    owned_tokens = tokens_win // (count_row * count_col)
    moved = (
        lax.all_to_all(query_index, ("row", "col"), split_axis=2, concat_axis=0, tiled=True),
        lax.all_to_all(key_index, ("row", "col"), split_axis=2, concat_axis=0, tiled=True),
        lax.all_to_all(window_out, ("row", "col"), split_axis=2, concat_axis=0, tiled=True),
    )
    owner_shape = moved[0].shape
    across = (-1, owned_tokens, HEADS, HEAD_DIM)
    index_out = index_attend(
        moved[0].reshape(across), moved[1].reshape(across), moved[2].reshape(across)
    )
    index_rows = index_out.reshape(-1, features)
    owner_rows = (
        jnp.dot(index_rows, proj_weight, preferred_element_type=jnp.float32) + proj_bias
    ).astype(jnp.bfloat16)
    last = owner_rows.shape[-1]
    shaped = owner_rows.reshape(tuple(owner_shape[:-1]) + (last,))
    returned = lax.all_to_all(shaped, ("row", "col"), split_axis=0, concat_axis=2, tiled=True)
    projected = returned.reshape(rows_dev * cols_dev * tokens_win, last)
    grouped = projected.reshape(rows_dev, cols_dev, TILE_ROWS, TILE_COLS, 2, 2, CHANNELS)
    shuffled = jnp.transpose(grouped, (0, 2, 4, 1, 3, 5, 6)).reshape(
        rows_dev * TILE_ROWS * 2, cols_dev * TILE_COLS * 2, CHANNELS
    )
    activated = jax.nn.gelu(convolve(shuffled, first_kernel, first_bias)).astype(jnp.bfloat16)
    return convolve(activated, second_kernel, second_bias).astype(jnp.bfloat16)


def solution(mesh):
    in_specs = (
        P(("grp", "row"), "col", None, None),
        P(("grp", "row"), "col", None, None),
        P(("grp", "row"), "col", None, None),
        P(("grp", "row"), "col", None, None),
        P(("grp", "row"), "col", None, None),
        P(),
        P(),
        P(),
        P(),
        P(),
        P(),
    )
    out_specs = P(("grp", "row"), "col", None)
    return jax.shard_map(shards, mesh=mesh, in_specs=in_specs, out_specs=out_specs, check_vma=False)
```

profile of v0, /device:TPU:17, one launch (start us, length us, event | category | flops | bytes accessed | tf_op | source)
XLA Modules:
  0.0 240.2 jit_solution(4875045535725694193)
XLA Ops:
  0.0 2.6 %copy.35 = bf16[1,4,128,1280]{2,3,1,0:T(8,128)(2,1)} copy(bf16[1,4,128,1280]{3,2,1,0:T(8,128)(2,1)} %param.13) | data formatting | bytes 2621440 | tf_op args[2]
  2.6 2.4 %copy.33 = bf16[1,4,128,1280]{2,3,1,0:T(8,128)(2,1)} copy(bf16[1,4,128,1280]{3,2,1,0:T(8,128)(2,1)} %param.11) | data formatting | bytes 2621440 | tf_op args[0]
  5.0 2.4 %copy.34 = bf16[1,4,128,1280]{2,3,1,0:T(8,128)(2,1)} copy(bf16[1,4,128,1280]{3,2,1,0:T(8,128)(2,1)} %param.12) | data formatting | bytes 2621440 | tf_op args[1]
  7.4 2.5 %fusion.114 = f32[4,8,128,128]{2,3,1,0:T(8,128)S(1)} fusion(bf16[4,128,8,160]{1,3,2,0:T(8,128)(2,1)} %bitcast.137, bf16[4,128,8,160]{1,3,2,0:T(8,128)(2,1)} %bitcast.138), kind=kOutput, calls=%fused_computation.150 | convolution fusion | flops 167772160 | bytes 4718592 | tf_op jit(solution)/shard_map/blhd,bmhd->bhlm/dot_general | solution.py:35
  9.9 1.3 copy-done.4
  11.2 0.5 fusion.112
  11.8 3.9 %convolution_convert_fusion = bf16[4,8,128,160]{2,3,1,0:T(8,128)(2,1)} fusion(bf16[4,128,8,160]{1,3,2,0:T(8,128)(2,1)} %bitcast.160, f32[4,8,128]{2,1,0:T(8,128)S(1)} %fusion.112, f32[4,8,128,128]{2,3,1,0:T(8,128)} %copy-done.4), kind=kOutput, calls=%fused_computation.58 | convolution fusion | flops 170528896 | bytes 4734976 | tf_op jit(solution)/shard_map/bhlm,bmhd->blhd/dot_general | solution.py:39
  15.7 3.7 %copy.37 = bf16[1,4,128,1280]{3,1,0,2:T(4,128)(2,1)} copy(bf16[1,4,128,1280]{2,3,1,0:T(8,128)(2,1)} %bitcast.161) | data formatting | bytes 2621440 | tf_op jit(solution)/shard_map/reshape | solution.py:86
  19.4 6.5 %all-to-all-start = ((bf16[1,4,128,1280]{3,1,0,2:T(4,128)(2,1)}), bf16[1,4,128,1280]{3,1,0,2:T(4,128)(2,1)}, u32[]{:S(2)}, u32[]{:S(2)}) async-start(bf16[1,4,128,1280]{3,1,0,2:T(4,128)(2,1)} %copy.37), calls=%async_computation | async-start | bytes 2621440 | tf_op jit(solution)/shard_map/all_to_all | solution.py:93
  25.9 3.4 %copy.42 = bf16[1,4,128,1280]{3,1,0,2:T(4,128)(2,1)} copy(bf16[1,4,128,1280]{3,2,1,0:T(8,128)(2,1)} %param.15) | data formatting | bytes 2621440 | tf_op args[4]
  29.3 26.9 %all-to-all-done = bf16[1,4,128,1280]{3,1,0,2:T(4,128)(2,1)} async-done(((bf16[1,4,128,1280]{3,1,0,2:T(4,128)(2,1)}), bf16[1,4,128,1280]{3,1,0,2:T(4,128)(2,1)}, u32[]{:S(2)}, u32[]{:S(2)}) %all-to-all-start) | async-done | bytes 1310752 | tf_op jit(solution)/shard_map/all_to_all | solution.py:93
  56.2 5.1 %all-to-all-start.2 = ((bf16[1,4,128,1280]{3,1,0,2:T(4,128)(2,1)}), bf16[1,4,128,1280]{3,1,0,2:T(4,128)(2,1)}, u32[]{:S(2)}, u32[]{:S(2)}) async-start(bf16[1,4,128,1280]{3,1,0,2:T(4,128)(2,1)} %copy.42), calls=%async_computation.2 | async-start | bytes 2621440 | tf_op jit(solution)/shard_map/all_to_all | solution.py:92
  61.3 3.4 %copy.40 = bf16[1,4,128,1280]{3,1,0,2:T(4,128)(2,1)} copy(bf16[1,4,128,1280]{3,2,1,0:T(8,128)(2,1)} %param.14) | data formatting | bytes 2621440 | tf_op args[3]
  64.7 26.9 %all-to-all-done.2 = bf16[1,4,128,1280]{3,1,0,2:T(4,128)(2,1)} async-done(((bf16[1,4,128,1280]{3,1,0,2:T(4,128)(2,1)}), bf16[1,4,128,1280]{3,1,0,2:T(4,128)(2,1)}, u32[]{:S(2)}, u32[]{:S(2)}) %all-to-all-start.2) | async-done | bytes 1310752 | tf_op jit(solution)/shard_map/all_to_all | solution.py:92
  91.6 5.1 %all-to-all-start.1 = ((bf16[1,4,128,1280]{3,1,0,2:T(4,128)(2,1)}), bf16[1,4,128,1280]{3,1,0,2:T(4,128)(2,1)}, u32[]{:S(2)}, u32[]{:S(2)}) async-start(bf16[1,4,128,1280]{3,1,0,2:T(4,128)(2,1)} %copy.40), calls=%async_computation.1 | async-start | bytes 2621440 | tf_op jit(solution)/shard_map/all_to_all | solution.py:91
  96.7 1.4 copy.67
  98.1 1.2 copy.39
  99.4 4.8 %reshape.99 = bf16[64,8,8,160]{3,2,1,0:T(8,128)(2,1)} reshape(bf16[16,1,4,8,1280]{4,3,2,0,1:T(8,128)(2,1)} %copy.39) | data formatting | bytes 2621440 | tf_op jit(solution)/shard_map/reshape | solution.py:98
  104.2 2.5 %copy.65 = bf16[1,4,16,8,1280]{4,3,1,2,0:T(8,128)(2,1)} copy(bf16[1,4,16,8,1280]{4,1,3,2,0:T(4,128)(2,1)} %bitcast.9) | data formatting | bytes 2621440 | tf_op jit(solution)/shard_map/all_to_all | solution.py:92
  106.8 4.8 %reshape.101 = bf16[64,8,8,160]{3,2,1,0:T(8,128)(2,1)} reshape(bf16[16,1,4,8,1280]{4,3,2,0,1:T(8,128)(2,1)} %bitcast.140) | data formatting | bytes 2621440 | tf_op jit(solution)/shard_map/reshape | solution.py:98
  111.6 15.4 %all-to-all-done.1 = bf16[1,4,128,1280]{3,1,0,2:T(4,128)(2,1)} async-done(((bf16[1,4,128,1280]{3,1,0,2:T(4,128)(2,1)}), bf16[1,4,128,1280]{3,1,0,2:T(4,128)(2,1)}, u32[]{:S(2)}, u32[]{:S(2)}) %all-to-all-start.1) | async-done | bytes 1310752 | tf_op jit(solution)/shard_map/all_to_all | solution.py:91
  127.0 2.5 %copy.66 = bf16[1,4,16,8,1280]{4,3,1,2,0:T(8,128)(2,1)} copy(bf16[1,4,16,8,1280]{4,1,3,2,0:T(4,128)(2,1)} %bitcast.7) | data formatting | bytes 2621440 | tf_op jit(solution)/shard_map/all_to_all | solution.py:91
  129.5 4.8 %reshape.100 = bf16[64,8,8,160]{3,2,1,0:T(8,128)(2,1)} reshape(bf16[16,1,4,8,1280]{4,3,2,0,1:T(8,128)(2,1)} %bitcast.141) | data formatting | bytes 2621440 | tf_op jit(solution)/shard_map/reshape | solution.py:98
  134.4 4.6 %fusion.26 = f32[8,8,64,64]{2,3,1,0:T(8,128)S(1)} fusion(bf16[64,8,8,160]{3,2,1,0:T(8,128)(2,1)} %reshape.101, bf16[64,8,8,160]{3,2,1,0:T(8,128)(2,1)} %reshape.100), kind=kOutput, calls=%fused_computation.41 | convolution fusion | flops 83886080 | bytes 3670016 | tf_op jit(solution)/shard_map/lbhd,mbhd->bhlm/dot_general | solution.py:45
  139.0 1.3 copy-done.3
  140.3 0.6 fusion.113
  141.0 5.6 %convert_bitcast_fusion = bf16[64,8,8,160]{3,0,2,1:T(8,128)(2,1)} fusion(bf16[64,8,8,160]{3,2,1,0:T(8,128)(2,1)} %reshape.99, f32[8,8,64]{2,1,0:T(8,128)S(1)} %fusion.113, f32[8,8,64,64]{2,3,1,0:T(8,128)} %copy-done.3), kind=kOutput, calls=%fused_computation.45 | convolution fusion | flops 85594176 | bytes 3686400 | tf_op jit(solution)/shard_map/bhlm,mbhd->lbhd/dot_general | solution.py:49
  146.6 4.1 %copy.48 = bf16[64,8,8,160]{3,2,1,0:T(8,128)(2,1)} copy(bf16[64,8,8,160]{3,0,2,1:T(8,128)(2,1)} %convert_bitcast_fusion) | data formatting | bytes 2621440 | tf_op jit(solution)/shard_map/convert_element_type | solution.py:51
  150.7 4.6 %reshape.102 = bf16[512,1280]{1,0:T(8,128)(2,1)} reshape(bf16[64,8,8,160]{3,2,1,0:T(8,128)(2,1)} %copy.48) | data formatting | bytes 2621440 | tf_op jit(solution)/shard_map/reshape | solution.py:100
  155.3 2.8 %add_convert_fusion = bf16[512,1024]{1,0:T(8,128)(2,1)S(1)} fusion(bf16[512,1280]{1,0:T(8,128)(2,1)} %reshape.102, bf16[1280,1024]{1,0:T(8,128)(2,1)S(1)} %copy-done, f32[1024]{0:T(1024)S(1)} %copy-done.9), kind=kOutput, calls=%fused_computation.44 | convolution fusion | flops 1343225856 | bytes 4984832 | tf_op jit(solution)/shard_map/dot_general | solution.py:102
  158.1 29.3 %all_to_all.60 = bf16[16,4,8,1024]{3,2,1,0:T(8,128)(2,1)S(1)} all-to-all(bf16[16,4,8,1024]{3,2,1,0:T(8,128)(2,1)S(1)} %bitcast.162), channel_id=1, replica_groups=mesh['grp'=2,'row'=8,'col'=2] {'row','col'}, dimensions={0} | all-to-all | bytes 2097152 | tf_op jit(solution)/shard_map/all_to_all | solution.py:106
  187.5 1.6 reshape_reshape.6
  189.1 2.4 copy.50
  191.5 0.4 reshape.104
  191.9 1.9 collective-permute-start
  193.9 1.2 reshape_reshape.7
  195.1 4.2 %collective-permute-start.1 = (bf16[1,128,256]{2,1,0:T(8,128)(2,1)S(1)}, bf16[1,128,256]{2,1,0:T(8,128)(2,1)S(1)}, u32[]{:S(2)}, u32[]{:S(2)}) collective-permute-start(bf16[1,128,256]{2,1,0:T(8,128)(2,1)S(1)} %get-tuple-element.33), channel_id=1, source_target_pairs={{2,0},{4,2},{6,4},{8,6},{10,8},{12,10},{14,12},{3,1},{5,3},{7,5},{... | collective-permute-start | bytes 196616 | tf_op jit(solution)/shard_map/ppermute | solution.py:23
  199.4 1.3 collective-permute-done.1
  201.0 1.3 collective-permute-start.2
  202.3 4.2 %collective-permute-start.3 = (bf16[18,1,256]{2,1,0:T(2,128)(2,1)S(1)}, bf16[18,1,256]{2,1,0:T(2,128)(2,1)S(1)}, u32[]{:S(2)}, u32[]{:S(2)}) collective-permute-start(bf16[18,1,256]{2,1,0:T(2,128)(2,1)S(1)} %get-tuple-element.25), channel_id=1, source_target_pairs={{1,0},{3,2},{5,4},{7,6},{9,8},{11,10},{13,12},{15,14},{17,16},{19,... | collective-permute-start | bytes 27656 | tf_op jit(solution)/shard_map/ppermute | solution.py:23
  207.4 3.7 %pad_maximum_fusion.5 = (bf16[16,128,256]{2,1,0:T(8,128)(2,1)S(1)}, bf16[16,128,256]{2,1,0:T(8,128)(2,1)S(1)}, bf16[16,128,256]{2,1,0:T(8,128)(2,1)S(1)}, bf16[1...) fusion(bf16[18,128,256]{2,1,0:T(8,128)(2,1)S(1)} %constant_dynamic-update-slice_, ...), kind=kLoop, calls=%fused_computation.76 | loop fusion | flops 12582912 | bytes 7489536 | tf_op jit(solution)/shard_map/concatenate | solution.py:24
  211.5 0.4 convolution_add_fusion.12
  212.0 0.4 convolution_add_fusion.11
  212.4 0.4 convolution_add_fusion.10
  212.9 0.8 copy-done.2
  213.6 0.4 convolution_add_fusion.9
  214.8 0.7 fusion.6
  215.4 0.7 fusion.15
  216.1 4.9 %collective-permute-start.5 = (bf16[1,128,256]{2,1,0:T(8,128)(2,1)S(1)}, bf16[1,128,256]{2,1,0:T(8,128)(2,1)S(1)}, u32[]{:S(2)}, u32[]{:S(2)}) collective-permute-start(bf16[1,128,256]{2,1,0:T(8,128)(2,1)S(1)} %get-tuple-element.29), channel_id=1, source_target_pairs={{2,0},{4,2},{6,4},{8,6},{10,8},{12,10},{14,12},{3,1},{5,3},{7,5},{... | collective-permute-start | bytes 196616 | tf_op jit(solution)/shard_map/ppermute | solution.py:23
  221.0 2.1 collective-permute-start.4
  223.1 4.0 %collective-permute-done.4 = bf16[1,128,256]{2,1,0:T(8,128)(2,1)S(1)} collective-permute-done((bf16[1,128,256]{2,1,0:T(8,128)(2,1)S(1)}, bf16[1,128,256]{2,1,0:T(8,128)(2,1)S(1)}, u32[]{:S(2)}, u32[]{:S(2)}) %collective-permute-start.4) | collective-permute-done | bytes 65568 | tf_op jit(solution)/shard_map/ppermute | solution.py:22
  227.1 1.3 collective-permute-start.6
  228.4 3.8 %collective-permute-start.7 = (bf16[18,1,256]{2,1,0:T(2,128)(2,1)S(1)}, bf16[18,1,256]{2,1,0:T(2,128)(2,1)S(1)}, u32[]{:S(2)}, u32[]{:S(2)}) collective-permute-start(bf16[18,1,256]{2,1,0:T(2,128)(2,1)S(1)} %get-tuple-element.20), channel_id=1, source_target_pairs={{1,0},{3,2},{5,4},{7,6},{9,8},{11,10},{13,12},{15,14},{17,16},{19,... | collective-permute-start | bytes 27656 | tf_op jit(solution)/shard_map/ppermute | solution.py:23
  232.4 0.4 fusion.54
  232.9 0.8 maximum_maximum_fusion
  233.7 1.0 fusion.107
  234.7 0.4 fusion.46
  235.1 0.4 convolution_add_fusion.6
  235.6 0.4 convolution_add_fusion.5
  236.0 0.5 convolution_add_fusion.4
  236.5 0.9 convolution_add_fusion.3
  237.3 0.5 convolution_add_fusion.2
  237.8 0.4 convolution_add_fusion.1
  238.5 1.5 fusion.7
  (36 shorter events, 3.0 us)
Async XLA Ops:
  0.0 155.3 %copy-start = (bf16[1280,1024]{1,0:T(8,128)(2,1)S(1)}, bf16[1280,1024]{1,0:T(8,128)(2,1)}, u32[]{:S(2)}) copy-start(bf16[1280,1024]{1,0:T(8,128)(2,1)} %param.16) | copy-start | bytes 7864324
  9.9 1.3 copy-start.4
  19.4 36.8 %all-to-all-start = ((bf16[1,4,128,1280]{3,1,0,2:T(4,128)(2,1)}), bf16[1,4,128,1280]{3,1,0,2:T(4,128)(2,1)}, u32[]{:S(2)}, u32[]{:S(2)}) async-start(bf16[1,4,128,1280]{3,1,0,2:T(4,128)(2,1)} %copy.37), calls=%async_computation | async-start | bytes 2621440 | tf_op jit(solution)/shard_map/all_to_all | solution.py:93
  56.2 35.4 %all-to-all-start.2 = ((bf16[1,4,128,1280]{3,1,0,2:T(4,128)(2,1)}), bf16[1,4,128,1280]{3,1,0,2:T(4,128)(2,1)}, u32[]{:S(2)}, u32[]{:S(2)}) async-start(bf16[1,4,128,1280]{3,1,0,2:T(4,128)(2,1)} %copy.42), calls=%async_computation.2 | async-start | bytes 2621440 | tf_op jit(solution)/shard_map/all_to_all | solution.py:92
  91.6 35.4 %all-to-all-start.1 = ((bf16[1,4,128,1280]{3,1,0,2:T(4,128)(2,1)}), bf16[1,4,128,1280]{3,1,0,2:T(4,128)(2,1)}, u32[]{:S(2)}, u32[]{:S(2)}) async-start(bf16[1,4,128,1280]{3,1,0,2:T(4,128)(2,1)} %copy.40), calls=%async_computation.1 | async-start | bytes 2621440 | tf_op jit(solution)/shard_map/all_to_all | solution.py:91
  139.0 1.3 copy-start.3
  150.7 4.6 %copy-start.9 = (f32[1024]{0:T(1024)S(1)}, f32[1024]{0:T(1024)}, u32[]{:S(2)}) copy-start(f32[1024]{0:T(1024)} %param.17) | copy-start | bytes 12292
  191.9 7.4 %collective-permute-start = (bf16[1,128,256]{2,1,0:T(8,128)(2,1)S(1)}, bf16[1,128,256]{2,1,0:T(8,128)(2,1)S(1)}, u32[]{:S(2)}, u32[]{:S(2)}) collective-permute-start(bf16[1,128,256]{2,1,0:T(8,128)(2,1)S(1)} %get-tuple-element.34), channel_id=1, source_target_pairs={{0,2},{2,4},{4,6},{6,8},{8,10},{10,12},{12,14},{1,3},{3,5},{5,7},{... | collective-permute-start | bytes 196616 | tf_op jit(solution)/shard_map/ppermute | solution.py:22
  195.1 5.6 %collective-permute-start.1 = (bf16[1,128,256]{2,1,0:T(8,128)(2,1)S(1)}, bf16[1,128,256]{2,1,0:T(8,128)(2,1)S(1)}, u32[]{:S(2)}, u32[]{:S(2)}) collective-permute-start(bf16[1,128,256]{2,1,0:T(8,128)(2,1)S(1)} %get-tuple-element.33), channel_id=1, source_target_pairs={{2,0},{4,2},{6,4},{8,6},{10,8},{12,10},{14,12},{3,1},{5,3},{7,5},{... | collective-permute-start | bytes 196616 | tf_op jit(solution)/shard_map/ppermute | solution.py:23
  199.4 7.1 %copy-start.5 = (bf16[3,3,256,256]{3,2,1,0:T(8,128)(2,1)S(1)}, bf16[3,3,256,256]{3,2,1,0:T(8,128)(2,1)}, u32[]{:S(2)}) copy-start(bf16[3,3,256,256]{3,2,1,0:T(8,128)(2,1)} %param.18) | copy-start | bytes 3538948
  201.0 6.4 %collective-permute-start.2 = (bf16[18,1,256]{2,1,0:T(2,128)(2,1)S(1)}, bf16[18,1,256]{2,1,0:T(2,128)(2,1)S(1)}, u32[]{:S(2)}, u32[]{:S(2)}) collective-permute-start(bf16[18,1,256]{2,1,0:T(2,128)(2,1)S(1)} %get-tuple-element.24), channel_id=1, source_target_pairs={{0,1},{2,3},{4,5},{6,7},{8,9},{10,11},{12,13},{14,15},{16,17},{18,... | collective-permute-start | bytes 27656 | tf_op jit(solution)/shard_map/ppermute | solution.py:22
  202.3 5.1 %collective-permute-start.3 = (bf16[18,1,256]{2,1,0:T(2,128)(2,1)S(1)}, bf16[18,1,256]{2,1,0:T(2,128)(2,1)S(1)}, u32[]{:S(2)}, u32[]{:S(2)}) collective-permute-start(bf16[18,1,256]{2,1,0:T(2,128)(2,1)S(1)} %get-tuple-element.25), channel_id=1, source_target_pairs={{1,0},{3,2},{5,4},{7,6},{9,8},{11,10},{13,12},{15,14},{17,16},{19,... | collective-permute-start | bytes 27656 | tf_op jit(solution)/shard_map/ppermute | solution.py:23
  212.4 1.2 copy-start.2
  214.1 0.7 copy-start.7
  216.1 7.0 %collective-permute-start.5 = (bf16[1,128,256]{2,1,0:T(8,128)(2,1)S(1)}, bf16[1,128,256]{2,1,0:T(8,128)(2,1)S(1)}, u32[]{:S(2)}, u32[]{:S(2)}) collective-permute-start(bf16[1,128,256]{2,1,0:T(8,128)(2,1)S(1)} %get-tuple-element.29), channel_id=1, source_target_pairs={{2,0},{4,2},{6,4},{8,6},{10,8},{12,10},{14,12},{3,1},{5,3},{7,5},{... | collective-permute-start | bytes 196616 | tf_op jit(solution)/shard_map/ppermute | solution.py:23
  221.0 11.4 %copy-start.6 = (bf16[3,3,256,256]{3,2,1,0:T(8,128)(2,1)S(1)}, bf16[3,3,256,256]{3,2,1,0:T(8,128)(2,1)}, u32[]{:S(2)}) copy-start(bf16[3,3,256,256]{3,2,1,0:T(8,128)(2,1)} %param.20) | copy-start | bytes 3538948
  221.0 6.0 %collective-permute-start.4 = (bf16[1,128,256]{2,1,0:T(8,128)(2,1)S(1)}, bf16[1,128,256]{2,1,0:T(8,128)(2,1)S(1)}, u32[]{:S(2)}, u32[]{:S(2)}) collective-permute-start(bf16[1,128,256]{2,1,0:T(8,128)(2,1)S(1)} %get-tuple-element.28), channel_id=1, source_target_pairs={{0,2},{2,4},{4,6},{6,8},{8,10},{10,12},{12,14},{1,3},{3,5},{5,7},{... | collective-permute-start | bytes 196616 | tf_op jit(solution)/shard_map/ppermute | solution.py:22
  227.1 5.8 %collective-permute-start.6 = (bf16[18,1,256]{2,1,0:T(2,128)(2,1)S(1)}, bf16[18,1,256]{2,1,0:T(2,128)(2,1)S(1)}, u32[]{:S(2)}, u32[]{:S(2)}) collective-permute-start(bf16[18,1,256]{2,1,0:T(2,128)(2,1)S(1)} %get-tuple-element.19), channel_id=1, source_target_pairs={{0,1},{2,3},{4,5},{6,7},{8,9},{10,11},{12,13},{14,15},{16,17},{18,... | collective-permute-start | bytes 27656 | tf_op jit(solution)/shard_map/ppermute | solution.py:22
  228.4 4.5 %collective-permute-start.7 = (bf16[18,1,256]{2,1,0:T(2,128)(2,1)S(1)}, bf16[18,1,256]{2,1,0:T(2,128)(2,1)S(1)}, u32[]{:S(2)}, u32[]{:S(2)}) collective-permute-start(bf16[18,1,256]{2,1,0:T(2,128)(2,1)S(1)} %get-tuple-element.20), channel_id=1, source_target_pairs={{1,0},{3,2},{5,4},{7,6},{9,8},{11,10},{13,12},{15,14},{17,16},{19,... | collective-permute-start | bytes 27656 | tf_op jit(solution)/shard_map/ppermute | solution.py:23
  237.8 0.7 copy-start.8
  238.3 1.9 copy-start.1
where the time goes:
time: 242 us; the launch traced here: 240 us
  waiting for transfers between devices  74.4 us (31%)
  local copies, waits for them, and re-layouts  59.8 us (25%)
  starting transfers between devices  40.4 us (17%)
  blocking collectives  29.3 us (12%)
  matrix products  29 us (12%)
  other arithmetic  6.82 us (3%)
    all_to_all x1, blocking collectives, shards(): lax.all_to_all(shaped, ('row', 'col'), split_axis=0, concat_axis=2, tiled...  29.3 us
    all_to_all x1, waiting for transfers between devices, shards(): lax.all_to_all(key_index, ('row', 'col'), split_axis=2, concat_axis=0, ti...  26.9 us
    all_to_all x1, waiting for transfers between devices, shards(): lax.all_to_all(window_out, ('row', 'col'), split_axis=2, concat_axis=0, t...  26.9 us
    unnamed x26, local copies, waits for them, and re-layouts  18.4 us
    ppermute x4, starting transfers between devices, extended(): after = lax.ppermute(first, axis, down)  17.2 us
    all_to_all x1, waiting for transfers between devices, shards(): lax.all_to_all(query_index, ('row', 'col'), split_axis=2, concat_axis=0,...  15.4 us
    dot_general x18, matrix products, convolve(): jnp.dot(cells, kernel[row_shift, col_shift], preferred_element_type=jnp.f...  9.55 us
    ppermute x4, starting transfers between devices, extended(): before = lax.ppermute(last, axis, up)  6.56 us
  transfers between devices with their start and end apart: 11, of which 5 were waited for; matrix products, arithmetic and copies ran while one was open for 10% of the time, Pallas kernels for 0%

commit v1 on v0

--- a/solution.py
+++ b/solution.py
@@ -1,8 +1,11 @@
+import functools
 import math
 
 import jax
 import jax.numpy as jnp
 from jax import lax
+from jax.experimental import pallas as pl
+from jax.experimental.pallas import tpu as pltpu
 from jax.sharding import PartitionSpec as P
 
 HEADS = 8
@@ -10,6 +13,7 @@
 CHANNELS = 256
 TILE_ROWS = 8
 TILE_COLS = 16
+LANES = 128
 
 
 def extended(value, sides, width):
@@ -64,6 +68,295 @@
                 cells, kernel[row_shift, col_shift], preferred_element_type=jnp.float32
             )
     return (total + bias).reshape(height, breadth, -1)
+
+
+def attend_heads(queries, key_part, value_part, same):
+    rows, features = queries.shape
+    head_dim = features // HEADS
+    factor = math.log2(math.e) / math.sqrt(head_dim)
+    blocks = [None] * (features // LANES)
+    for head in range(HEADS):
+        low, high = (head * head_dim, (head + 1) * head_dim)
+        start, stop = (low // LANES * LANES, -(-high // LANES) * LANES)
+        lane = lax.broadcasted_iota(jnp.int32, (rows, stop - start), 1) + start
+        inside = (lane >= low) & (lane < high)
+        part = queries[:, start:stop]
+        part = jnp.where(inside, part, jnp.zeros_like(part))
+        scores = lax.dot_general(
+            part,
+            key_part(start, stop),
+            (((1,), (1,)), ((), ())),
+            preferred_element_type=jnp.float32,
+        )
+        if same is not None:
+            scores = jnp.where(same, scores, -1e30)
+        highest = jnp.max(scores, axis=-1, keepdims=True)
+        raised = jnp.exp2((scores - highest) * factor)
+        weights = (raised * (1.0 / jnp.sum(raised, axis=-1, keepdims=True))).astype(jnp.bfloat16)
+        mixed = jnp.dot(weights, value_part(start, stop), preferred_element_type=jnp.float32)
+        mixed = jnp.where(inside, mixed, 0.0)
+        for block in range(start // LANES, stop // LANES):
+            piece = mixed[:, block * LANES - start : (block + 1) * LANES - start]
+            blocks[block] = piece if blocks[block] is None else blocks[block] + piece
+    return jnp.concatenate(blocks, axis=1).astype(jnp.bfloat16)
+
+
+def attention_kernel(
+    count_row,
+    count_col,
+    qw_hbm,
+    kw_hbm,
+    vw_hbm,
+    qi_hbm,
+    ki_hbm,
+    pw_hbm,
+    pb_ref,
+    out_hbm,
+    qw,
+    kw,
+    vw,
+    pw,
+    window_out,
+    k_all,
+    v_all,
+    q_all,
+    proj,
+    load_sem,
+    own_sem,
+    q_own_sem,
+    out_own_sem,
+    k_send,
+    k_recv,
+    v_send,
+    v_recv,
+    q_send,
+    q_recv,
+    r_send,
+    r_recv,
+):
+    count = count_row * count_col
+    windows = qw.shape[0]
+    owned = k_all.shape[2]
+    features = qw.shape[2]
+    me = lax.axis_index("row") * count_col + lax.axis_index("col")
+
+    def offset(step):
+        half = (step + 1) // 2
+        return count // 2 + jnp.where(step % 2 == 1, half, -half)
+
+    def peer_of(shift):
+        return lax.rem(me + shift, count)
+
+    def device(peer):
+        return {"row": peer // count_col, "col": lax.rem(peer, count_col)}
+
+    def tokens(peer):
+        return pl.ds(pl.multiple_of(peer * owned, owned), owned)
+
+    def copy_k(shift):
+        peer = peer_of(shift)
+        return pltpu.make_async_remote_copy(
+            src_ref=ki_hbm.at[:, tokens(peer), :],
+            dst_ref=k_all.at[me],
+            send_sem=k_send.at[shift],
+            recv_sem=k_recv.at[shift],
+            device_id=device(peer),
+            device_id_type=pl.DeviceIdType.MESH,
+        )
+
+    def copy_v(shift):
+        peer = peer_of(shift)
+        return pltpu.make_async_remote_copy(
+            src_ref=window_out.at[:, tokens(peer), :],
+            dst_ref=v_all.at[me],
+            send_sem=v_send.at[shift],
+            recv_sem=v_recv.at[shift],
+            device_id=device(peer),
+            device_id_type=pl.DeviceIdType.MESH,
+        )
+
+    def copy_q(window, shift):
+        peer = peer_of(shift)
+        return pltpu.make_async_remote_copy(
+            src_ref=qi_hbm.at[window, tokens(peer), :],
+            dst_ref=q_all.at[window, me],
+            send_sem=q_send.at[window, shift],
+            recv_sem=q_recv.at[window, shift],
+            device_id=device(peer),
+            device_id_type=pl.DeviceIdType.MESH,
+        )
+
+    def copy_r(window, shift):
+        peer = peer_of(shift)
+        return pltpu.make_async_remote_copy(
+            src_ref=proj.at[window, tokens(peer), :],
+            dst_ref=out_hbm.at[window, tokens(me), :],
+            send_sem=r_send.at[window, shift],
+            recv_sem=r_recv.at[window, shift],
+            device_id=device(peer),
+            device_id_type=pl.DeviceIdType.MESH,
+        )
+
+    def own_q(window):
+        return pltpu.make_async_copy(
+            qi_hbm.at[window, tokens(me), :], q_all.at[window, me], q_own_sem.at[window]
+        )
+
+    def own_r(window):
+        return pltpu.make_async_copy(
+            proj.at[window, tokens(me), :],
+            out_hbm.at[window, tokens(me), :],
+            out_own_sem.at[window],
+        )
+
+    loads = [
+        pltpu.make_async_copy(source, target, load_sem.at[place])
+        for place, (source, target) in enumerate(
+            ((qw_hbm, qw), (kw_hbm, kw), (vw_hbm, vw), (pw_hbm, pw))
+        )
+    ]
+    for load in loads:
+        load.start()
+    own_k = pltpu.make_async_copy(ki_hbm.at[:, tokens(me), :], k_all.at[me], own_sem.at[0])
+    own_k.start()
+
+    def each_shift(body):
+        def step(index, carry):
+            body(offset(index))
+            return carry
+
+        lax.fori_loop(0, count - 1, step, 0)
+
+    def each_window(body):
+        def step(index, carry):
+            body(index)
+            return carry
+
+        lax.fori_loop(0, windows, step, 0)
+
+    each_window(lambda window: own_q(window).start())
+
+    barrier = pltpu.get_barrier_semaphore()
+
+    def greet(shift):
+        pl.semaphore_signal(
+            barrier,
+            inc=1,
+            device_id=device(peer_of(shift)),
+            device_id_type=pl.DeviceIdType.MESH,
+        )
+
+    each_shift(greet)
+    pl.semaphore_wait(barrier, count - 1)
+    each_shift(lambda shift: copy_k(shift).start())
+
+    for load in loads:
+        load.wait()
+
+    def within(window):
+        window_out[window] = attend_heads(
+            qw[window],
+            lambda start, stop: kw[window, :, start:stop],
+            lambda start, stop: vw[window, :, start:stop],
+            None,
+        )
+
+    each_window(within)
+    own_v = pltpu.make_async_copy(
+        window_out.at[:, tokens(me), :], v_all.at[me], own_sem.at[1]
+    )
+    own_v.start()
+    each_shift(lambda shift: copy_v(shift).start())
+    each_window(lambda window: each_shift(lambda shift: copy_q(window, shift).start()))
+
+    own_k.wait()
+    own_v.wait()
+    each_shift(lambda shift: copy_k(shift).wait())
+    each_shift(lambda shift: copy_v(shift).wait())
+
+    key_rows = k_all.reshape(count * windows * owned, features)
+    value_rows = v_all.reshape(count * windows * owned, features)
+    query_rows = q_all.reshape(windows, count * owned, features)
+    square = (count * owned, count * windows * owned)
+    same = lax.rem(lax.broadcasted_iota(jnp.int32, square, 0), owned) == lax.rem(
+        lax.broadcasted_iota(jnp.int32, square, 1), owned
+    )
+
+    def across(window):
+        own_q(window).wait()
+        each_shift(lambda shift: copy_q(window, shift).wait())
+        mixed = attend_heads(
+            query_rows[window],
+            lambda start, stop: key_rows[:, start:stop],
+            lambda start, stop: value_rows[:, start:stop],
+            same,
+        )
+        rows = jnp.dot(mixed, pw[...], preferred_element_type=jnp.float32) + pb_ref[...]
+        proj[window] = rows.astype(jnp.bfloat16)
+        own_r(window).start()
+        each_shift(lambda shift: copy_r(window, shift).start())
+
+    each_window(across)
+
+    def finish(window):
+        own_r(window).wait()
+        each_shift(lambda shift: copy_r(window, shift).wait())
+
+    each_window(finish)
+
+
+def attention_exchange(qw, kw, vw, qi, ki, proj_weight, proj_bias):
+    windows, tokens_win, features = qw.shape
+    count_row = lax.axis_size("row")
+    count_col = lax.axis_size("col")
+    count = count_row * count_col
+    owned = tokens_win // count
+    channels = proj_weight.shape[-1]
+    whole = pl.BlockSpec(memory_space=pl.ANY)
+    dma = pltpu.SemaphoreType.DMA
+    return pl.pallas_call(
+        functools.partial(attention_kernel, count_row, count_col),
+        out_shape=jax.ShapeDtypeStruct((windows, tokens_win, channels), jnp.bfloat16),
+        in_specs=[whole] * 6 + [pl.BlockSpec(memory_space=pltpu.VMEM)],
+        out_specs=whole,
+        scratch_shapes=[
+            pltpu.VMEM(qw.shape, jnp.bfloat16),
+            pltpu.VMEM(qw.shape, jnp.bfloat16),
+            pltpu.VMEM(qw.shape, jnp.bfloat16),
+            pltpu.VMEM(proj_weight.shape, jnp.bfloat16),
+            pltpu.VMEM(qw.shape, jnp.bfloat16),
+            pltpu.VMEM((count, windows, owned, features), jnp.bfloat16),
+            pltpu.VMEM((count, windows, owned, features), jnp.bfloat16),
+            pltpu.VMEM((windows, count, owned, features), jnp.bfloat16),
+            pltpu.VMEM((windows, tokens_win, channels), jnp.bfloat16),
+            dma((4,)),
+            dma((2,)),
+            dma((windows,)),
+            dma((windows,)),
+            dma((count,)),
+            dma((count,)),
+            dma((count,)),
+            dma((count,)),
+            dma((windows, count)),
+            dma((windows, count)),
+            dma((windows, count)),
+            dma((windows, count)),
+        ],
+        compiler_params=pltpu.CompilerParams(
+            collective_id=0, has_side_effects=True, vmem_limit_bytes=48 * 1024 * 1024
+        ),
+    )(qw, kw, vw, qi, ki, proj_weight, proj_bias.reshape(1, channels))
+
+
+def convolutions(
+    projected, rows_dev, cols_dev, first_kernel, first_bias, second_kernel, second_bias
+):
+    grouped = projected.reshape(rows_dev, cols_dev, TILE_ROWS, TILE_COLS, 2, 2, CHANNELS)
+    shuffled = jnp.transpose(grouped, (0, 2, 4, 1, 3, 5, 6)).reshape(
+        rows_dev * TILE_ROWS * 2, cols_dev * TILE_COLS * 2, CHANNELS
+    )
+    activated = jax.nn.gelu(convolve(shuffled, first_kernel, first_bias)).astype(jnp.bfloat16)
+    return convolve(activated, second_kernel, second_bias).astype(jnp.bfloat16)
 
 
 def shards(
@@ -80,6 +373,21 @@
     second_bias,
 ):
     rows_dev, cols_dev, tokens_win, features = query_window.shape
+    flat = (rows_dev * cols_dev, tokens_win, features)
+    owners = lax.axis_size("row") * lax.axis_size("col")
+    if tokens_win % (owners * 8) == 0 and features % LANES == 0:
+        projected = attention_exchange(
+            query_window.reshape(flat),
+            key_window.reshape(flat),
+            value_window.reshape(flat),
+            query_index.reshape(flat),
+            key_index.reshape(flat),
+            proj_weight,
+            proj_bias,
+        )
+        return convolutions(
+            projected, rows_dev, cols_dev, first_kernel, first_bias, second_kernel, second_bias
+        )
     layout = (rows_dev * cols_dev, tokens_win, HEADS, HEAD_DIM)
     window_out = window_attend(
         query_window.reshape(layout), key_window.reshape(layout), value_window.reshape(layout)
@@ -105,12 +413,9 @@
     shaped = owner_rows.reshape(tuple(owner_shape[:-1]) + (last,))
     returned = lax.all_to_all(shaped, ("row", "col"), split_axis=0, concat_axis=2, tiled=True)
     projected = returned.reshape(rows_dev * cols_dev * tokens_win, last)
-    grouped = projected.reshape(rows_dev, cols_dev, TILE_ROWS, TILE_COLS, 2, 2, CHANNELS)
-    shuffled = jnp.transpose(grouped, (0, 2, 4, 1, 3, 5, 6)).reshape(
-        rows_dev * TILE_ROWS * 2, cols_dev * TILE_COLS * 2, CHANNELS
-    )
-    activated = jax.nn.gelu(convolve(shuffled, first_kernel, first_bias)).astype(jnp.bfloat16)
-    return convolve(activated, second_kernel, second_bias).astype(jnp.bfloat16)
+    return convolutions(
+        projected, rows_dev, cols_dev, first_kernel, first_bias, second_kernel, second_bias
+    )
 
 
 def solution(mesh):

time: 242 us -> 168 us (0.69)
  Pallas kernels: 0 us -> 116 us
  waiting for transfers between devices: 74.4 us -> 4.94 us
  local copies, waits for them, and re-layouts: 59.8 us -> 8.97 us
  blocking collectives: 29.3 us -> 0 us
  matrix products: 29 us -> 9.54 us
  starting transfers between devices: 40.4 us -> 22.9 us
    pallas_call x0 -> x1, Pallas kernels: none -> 116 us  [attention_exchange(): pl.pallas_call(functools.partial(attention_kernel, count_row, count_col),...]
    all_to_all x3 -> x0, waiting for transfers between devices: 69.2 us -> none  [the longest x1 26.9 us: shards(): lax.all_to_all(key_index, ('row', 'col'), split_axis=2, concat_axis=0, ti...]
    all_to_all x1 -> x0, blocking collectives: 29.3 us -> none  [shards(): lax.all_to_all(shaped, ('row', 'col'), split_axis=0, concat_axis=2, tiled...]
    reshape x6 -> x3, local copies, waits for them, and re-layouts: 23.3 us -> 2.4 us  [the longest x2 1.96 us: convolutions(): projected.reshape(rows_dev, cols_dev, TILE_ROWS, TILE_COLS, 2, 2, CHANNELS)]
    dot_general x5 -> x0, matrix products: 19.5 us -> none  [the longest x1 5.64 us: index_attend(): jnp.einsum('bhlm,mbhd->lbhd', weights, values, preferred_element_type=jnp...]
    all_to_all x3 -> x0, starting transfers between devices: 16.7 us -> none  [the longest x1 6.46 us: shards(): lax.all_to_all(window_out, ('row', 'col'), split_axis=2, concat_axis=0, t...]
    unnamed x26 -> x17, local copies, waits for them, and re-layouts: 18.4 us -> 5.11 us
    all_to_all x5 -> x0, local copies, waits for them, and re-layouts: 7.82 us -> none  [the longest x2 2.65 us: shards(): lax.all_to_all(window_out, ('row', 'col'), split_axis=2, concat_axis=0, t...]
  transfers between devices with their start and end apart: 11 -> 8, of which waited for: 5 -> 3; matrix products, arithmetic and copies ran while one was open for 10% -> 1% of each run, Pallas kernels for 0% -> 0%
where the time goes in v1:
time: 168 us
  Pallas kernels  116 us (69%)
  starting transfers between devices  22.9 us (14%)
  matrix products  9.54 us (6%)
  local copies, waits for them, and re-layouts  8.97 us (5%)
  other arithmetic  5.74 us (3%)
  waiting for transfers between devices  4.94 us (3%)
    pallas_call x1, Pallas kernels, attention_exchange(): pl.pallas_call(functools.partial(attention_kernel, count_row, count_col),...  116 us
    ppermute x4, starting transfers between devices, extended(): after = lax.ppermute(first, axis, down)  16.1 us
    dot_general x18, matrix products, convolve(): jnp.dot(cells, kernel[row_shift, col_shift], preferred_element_type=jnp.f...  9.54 us
    ppermute x4, starting transfers between devices, extended(): before = lax.ppermute(last, axis, up)  6.81 us
    unnamed x17, local copies, waits for them, and re-layouts  5.11 us
    concatenate x4, other arithmetic, extended(): value = jnp.concatenate([before, value, after], axis=dim)  5.04 us
    ppermute x4, waiting for transfers between devices, extended(): before = lax.ppermute(last, axis, up)  3.8 us
  transfers between devices with their start and end apart: 8, of which 3 were waited for; matrix products, arithmetic and copies ran while one was open for 1% of the time, Pallas kernels for 0%

profile of v1, /device:TPU:17, one launch (start us, length us, event | category | flops | bytes accessed | tf_op | source)
XLA Modules:
  0.0 168.0 jit_solution(5587278795805449052)
XLA Ops:
  0.0 0.0 copy-start
  0.0 1.3 copy-done
  1.3 0.0 copy-start.1
  1.3 1.3 copy-done.1
  2.6 0.0 copy-start.2
  2.6 1.3 copy-done.2
  4.0 0.0 copy-start.3
  4.0 0.7 copy-done.3
  4.6 115.5 %shard_map.109 = bf16[4,128,1024]{2,1,0:T(8,128)(2,1)S(1)} custom-call(bf16[4,128,1280]{2,1,0:T(8,128)(2,1)S(1)} %bitcast.98, bf16[4,128,1280]{2,1,0:T(8,128)(2,1)S(1)} %bitcast.99, bf16[4,128,1280]{2,1,0:T(8,128)(2,1)S(1)} %bitcast.100, bf16[4,128,1280]{2,1,0:T(8,128)(2,1)} %bitcast.121, bf16[4,128,1280]{2,1,0:T(8,128)(2,1)} %bitcast.122, ...), custom_call_target="tpu_custom_call" | custom-call | tf_op jit(solution)/shard_map/pallas_call | solution.py:317
  120.2 0.8 reshape.86
  121.0 1.2 copy.14
  122.1 0.4 reshape.87
  122.6 2.0 %collective-permute-start = (bf16[1,128,256]{2,1,0:T(8,128)(2,1)S(1)}, bf16[1,128,256]{2,1,0:T(8,128)(2,1)S(1)}, u32[]{:S(2)}, u32[]{:S(2)}) collective-permute-start(bf16[1,128,256]{2,1,0:T(8,128)(2,1)S(1)} %get-tuple-element.34), channel_id=1, source_target_pairs={{0,2},{2,4},{4,6},{6,8},{8,10},{10,12},{12,14},{1,3},{3,5},{5,7},{... | collective-permute-start | bytes 196616 | tf_op jit(solution)/shard_map/ppermute | solution.py:26
  124.6 4.2 %collective-permute-start.1 = (bf16[1,128,256]{2,1,0:T(8,128)(2,1)S(1)}, bf16[1,128,256]{2,1,0:T(8,128)(2,1)S(1)}, u32[]{:S(2)}, u32[]{:S(2)}) collective-permute-start(bf16[1,128,256]{2,1,0:T(8,128)(2,1)S(1)} %get-tuple-element.33), channel_id=1, source_target_pairs={{2,0},{4,2},{6,4},{8,6},{10,8},{12,10},{14,12},{3,1},{5,3},{7,5},{... | collective-permute-start | bytes 196616 | tf_op jit(solution)/shard_map/ppermute | solution.py:27
  128.8 0.4 reshape_reshape.3
  129.3 0.0 collective-permute-done
  129.3 0.0 copy-start.4
  129.3 0.9 collective-permute-done.1
  130.2 0.4 pad_maximum_fusion.6
  130.7 1.3 collective-permute-start.2
  132.0 3.9 %collective-permute-start.3 = (bf16[18,1,256]{2,1,0:T(2,128)(2,1)S(1)}, bf16[18,1,256]{2,1,0:T(2,128)(2,1)S(1)}, u32[]{:S(2)}, u32[]{:S(2)}) collective-permute-start(bf16[18,1,256]{2,1,0:T(2,128)(2,1)S(1)} %get-tuple-element.25), channel_id=1, source_target_pairs={{1,0},{3,2},{5,4},{7,6},{9,8},{11,10},{13,12},{15,14},{17,16},{19,... | collective-permute-start | bytes 27656 | tf_op jit(solution)/shard_map/ppermute | solution.py:27
  135.9 0.0 copy-done.4
  135.9 0.4 fusion.44
  136.3 0.4 fusion.51
  136.8 0.0 collective-permute-done.2
  136.8 0.0 collective-permute-done.3
  136.8 3.7 %pad_maximum_fusion.5 = (bf16[16,128,256]{2,1,0:T(8,128)(2,1)S(1)}, bf16[16,128,256]{2,1,0:T(8,128)(2,1)S(1)}, bf16[16,128,256]{2,1,0:T(8,128)(2,1)S(1)}, bf16[1...) fusion(bf16[18,128,256]{2,1,0:T(8,128)(2,1)S(1)} %constant_dynamic-update-slice_, ...), kind=kLoop, calls=%fused_computation.55 | loop fusion | flops 12582912 | bytes 7489536 | tf_op jit(solution)/shard_map/concatenate | solution.py:28
  140.5 0.4 fusion.42
  140.9 0.4 convolution_add_fusion.12
  141.4 0.4 convolution_add_fusion.11
  141.8 0.4 convolution_add_fusion.10
  142.2 0.4 convolution_add_fusion.9
  142.7 0.0 copy-start.6
  142.7 0.4 convolution_add_fusion.8
  143.1 0.2 copy-done.6
  143.4 0.6 fusion.4
  144.0 0.7 fusion.13
  144.7 4.4 %collective-permute-start.5 = (bf16[1,128,256]{2,1,0:T(8,128)(2,1)S(1)}, bf16[1,128,256]{2,1,0:T(8,128)(2,1)S(1)}, u32[]{:S(2)}, u32[]{:S(2)}) collective-permute-start(bf16[1,128,256]{2,1,0:T(8,128)(2,1)S(1)} %get-tuple-element.29), channel_id=1, source_target_pairs={{2,0},{4,2},{6,4},{8,6},{10,8},{12,10},{14,12},{3,1},{5,3},{7,5},{... | collective-permute-start | bytes 196616 | tf_op jit(solution)/shard_map/ppermute | solution.py:27
  149.1 0.0 copy-start.5
  149.1 2.2 %collective-permute-start.4 = (bf16[1,128,256]{2,1,0:T(8,128)(2,1)S(1)}, bf16[1,128,256]{2,1,0:T(8,128)(2,1)S(1)}, u32[]{:S(2)}, u32[]{:S(2)}) collective-permute-start(bf16[1,128,256]{2,1,0:T(8,128)(2,1)S(1)} %get-tuple-element.28), channel_id=1, source_target_pairs={{0,2},{2,4},{4,6},{6,8},{8,10},{10,12},{12,14},{1,3},{3,5},{5,7},{... | collective-permute-start | bytes 196616 | tf_op jit(solution)/shard_map/ppermute | solution.py:26
  151.4 0.0 collective-permute-done.5
  151.4 3.8 %collective-permute-done.4 = bf16[1,128,256]{2,1,0:T(8,128)(2,1)S(1)} collective-permute-done((bf16[1,128,256]{2,1,0:T(8,128)(2,1)S(1)}, bf16[1,128,256]{2,1,0:T(8,128)(2,1)S(1)}, u32[]{:S(2)}, u32[]{:S(2)}) %collective-permute-start.4) | collective-permute-done | bytes 65568 | tf_op jit(solution)/shard_map/ppermute | solution.py:26
  155.2 1.3 collective-permute-start.6
  156.5 3.6 %collective-permute-start.7 = (bf16[18,1,256]{2,1,0:T(2,128)(2,1)S(1)}, bf16[18,1,256]{2,1,0:T(2,128)(2,1)S(1)}, u32[]{:S(2)}, u32[]{:S(2)}) collective-permute-start(bf16[18,1,256]{2,1,0:T(2,128)(2,1)S(1)} %get-tuple-element.20), channel_id=1, source_target_pairs={{1,0},{3,2},{5,4},{7,6},{9,8},{11,10},{13,12},{15,14},{17,16},{19,... | collective-permute-start | bytes 27656 | tf_op jit(solution)/shard_map/ppermute | solution.py:27
  160.1 0.1 pad_maximum_fusion.1
  160.3 0.0 copy-done.5
  160.3 0.4 fusion.39
  160.7 0.0 collective-permute-done.6
  160.7 0.2 collective-permute-done.7
  160.9 0.8 maximum_maximum_fusion
  161.8 1.0 fusion.76
  162.8 0.4 fusion.31
  163.2 0.4 convolution_add_fusion.6
  163.6 0.4 convolution_add_fusion.5
  164.1 0.4 convolution_add_fusion.4
  164.5 0.9 convolution_add_fusion.3
  165.4 0.5 convolution_add_fusion.2
  165.9 0.0 copy-start.7
  165.9 0.4 convolution_add_fusion.1
  166.3 0.2 copy-done.7
  166.6 1.5 fusion.5
  (6 shorter events, 0.1 us)
Async XLA Ops:
  0.0 1.3 copy-start
  1.3 1.3 copy-start.1
  2.6 1.3 copy-start.2
  4.0 0.7 copy-start.3
  122.6 6.6 %collective-permute-start = (bf16[1,128,256]{2,1,0:T(8,128)(2,1)S(1)}, bf16[1,128,256]{2,1,0:T(8,128)(2,1)S(1)}, u32[]{:S(2)}, u32[]{:S(2)}) collective-permute-start(bf16[1,128,256]{2,1,0:T(8,128)(2,1)S(1)} %get-tuple-element.34), channel_id=1, source_target_pairs={{0,2},{2,4},{4,6},{6,8},{8,10},{10,12},{12,14},{1,3},{3,5},{5,7},{... | collective-permute-start | bytes 196616 | tf_op jit(solution)/shard_map/ppermute | solution.py:26
  124.6 5.6 %collective-permute-start.1 = (bf16[1,128,256]{2,1,0:T(8,128)(2,1)S(1)}, bf16[1,128,256]{2,1,0:T(8,128)(2,1)S(1)}, u32[]{:S(2)}, u32[]{:S(2)}) collective-permute-start(bf16[1,128,256]{2,1,0:T(8,128)(2,1)S(1)} %get-tuple-element.33), channel_id=1, source_target_pairs={{2,0},{4,2},{6,4},{8,6},{10,8},{12,10},{14,12},{3,1},{5,3},{7,5},{... | collective-permute-start | bytes 196616 | tf_op jit(solution)/shard_map/ppermute | solution.py:27
  129.3 6.6 %copy-start.4 = (bf16[3,3,256,256]{3,2,1,0:T(8,128)(2,1)S(1)}, bf16[3,3,256,256]{3,2,1,0:T(8,128)(2,1)}, u32[]{:S(2)}) copy-start(bf16[3,3,256,256]{3,2,1,0:T(8,128)(2,1)} %param.18) | copy-start | bytes 3538948
  130.7 6.1 %collective-permute-start.2 = (bf16[18,1,256]{2,1,0:T(2,128)(2,1)S(1)}, bf16[18,1,256]{2,1,0:T(2,128)(2,1)S(1)}, u32[]{:S(2)}, u32[]{:S(2)}) collective-permute-start(bf16[18,1,256]{2,1,0:T(2,128)(2,1)S(1)} %get-tuple-element.24), channel_id=1, source_target_pairs={{0,1},{2,3},{4,5},{6,7},{8,9},{10,11},{12,13},{14,15},{16,17},{18,... | collective-permute-start | bytes 27656 | tf_op jit(solution)/shard_map/ppermute | solution.py:26
  132.0 4.8 %collective-permute-start.3 = (bf16[18,1,256]{2,1,0:T(2,128)(2,1)S(1)}, bf16[18,1,256]{2,1,0:T(2,128)(2,1)S(1)}, u32[]{:S(2)}, u32[]{:S(2)}) collective-permute-start(bf16[18,1,256]{2,1,0:T(2,128)(2,1)S(1)} %get-tuple-element.25), channel_id=1, source_target_pairs={{1,0},{3,2},{5,4},{7,6},{9,8},{11,10},{13,12},{15,14},{17,16},{19,... | collective-permute-start | bytes 27656 | tf_op jit(solution)/shard_map/ppermute | solution.py:27
  142.7 0.7 copy-start.6
  144.7 6.7 %collective-permute-start.5 = (bf16[1,128,256]{2,1,0:T(8,128)(2,1)S(1)}, bf16[1,128,256]{2,1,0:T(8,128)(2,1)S(1)}, u32[]{:S(2)}, u32[]{:S(2)}) collective-permute-start(bf16[1,128,256]{2,1,0:T(8,128)(2,1)S(1)} %get-tuple-element.29), channel_id=1, source_target_pairs={{2,0},{4,2},{6,4},{8,6},{10,8},{12,10},{14,12},{3,1},{5,3},{7,5},{... | collective-permute-start | bytes 196616 | tf_op jit(solution)/shard_map/ppermute | solution.py:27
  149.1 11.1 %copy-start.5 = (bf16[3,3,256,256]{3,2,1,0:T(8,128)(2,1)S(1)}, bf16[3,3,256,256]{3,2,1,0:T(8,128)(2,1)}, u32[]{:S(2)}) copy-start(bf16[3,3,256,256]{3,2,1,0:T(8,128)(2,1)} %param.20) | copy-start | bytes 3538948
  149.1 6.0 %collective-permute-start.4 = (bf16[1,128,256]{2,1,0:T(8,128)(2,1)S(1)}, bf16[1,128,256]{2,1,0:T(8,128)(2,1)S(1)}, u32[]{:S(2)}, u32[]{:S(2)}) collective-permute-start(bf16[1,128,256]{2,1,0:T(8,128)(2,1)S(1)} %get-tuple-element.28), channel_id=1, source_target_pairs={{0,2},{2,4},{4,6},{6,8},{8,10},{10,12},{12,14},{1,3},{3,5},{5,7},{... | collective-permute-start | bytes 196616 | tf_op jit(solution)/shard_map/ppermute | solution.py:26
  155.2 5.5 %collective-permute-start.6 = (bf16[18,1,256]{2,1,0:T(2,128)(2,1)S(1)}, bf16[18,1,256]{2,1,0:T(2,128)(2,1)S(1)}, u32[]{:S(2)}, u32[]{:S(2)}) collective-permute-start(bf16[18,1,256]{2,1,0:T(2,128)(2,1)S(1)} %get-tuple-element.19), channel_id=1, source_target_pairs={{0,1},{2,3},{4,5},{6,7},{8,9},{10,11},{12,13},{14,15},{16,17},{18,... | collective-permute-start | bytes 27656 | tf_op jit(solution)/shard_map/ppermute | solution.py:26
  156.5 4.4 %collective-permute-start.7 = (bf16[18,1,256]{2,1,0:T(2,128)(2,1)S(1)}, bf16[18,1,256]{2,1,0:T(2,128)(2,1)S(1)}, u32[]{:S(2)}, u32[]{:S(2)}) collective-permute-start(bf16[18,1,256]{2,1,0:T(2,128)(2,1)S(1)} %get-tuple-element.20), channel_id=1, source_target_pairs={{1,0},{3,2},{5,4},{7,6},{9,8},{11,10},{13,12},{15,14},{17,16},{19,... | collective-permute-start | bytes 27656 | tf_op jit(solution)/shard_map/ppermute | solution.py:27
  165.9 0.7 copy-start.7

commit v2 on v1

--- a/solution.py
+++ b/solution.py
@@ -110,8 +110,12 @@
     qi_hbm,
     ki_hbm,
     pw_hbm,
+    fk_hbm,
+    sk_hbm,
     pb_ref,
-    out_hbm,
+    fb_ref,
+    sb_ref,
+    out_ref,
     qw,
     kw,
     vw,
@@ -121,6 +125,15 @@
     v_all,
     q_all,
     proj,
+    field,
+    fk,
+    sk,
+    halo_up,
+    halo_down,
+    side_right,
+    side_left,
+    shuffled,
+    activated,
     load_sem,
     own_sem,
     q_own_sem,
@@ -133,6 +146,10 @@
     q_recv,
     r_send,
     r_recv,
+    edge_send,
+    edge_recv,
+    side_send,
+    side_recv,
 ):
     count = count_row * count_col
     windows = qw.shape[0]
@@ -190,7 +207,7 @@
         peer = peer_of(shift)
         return pltpu.make_async_remote_copy(
             src_ref=proj.at[window, tokens(peer), :],
-            dst_ref=out_hbm.at[window, tokens(me), :],
+            dst_ref=field.at[window, tokens(me), :],
             send_sem=r_send.at[window, shift],
             recv_sem=r_recv.at[window, shift],
             device_id=device(peer),
@@ -205,14 +222,21 @@
     def own_r(window):
         return pltpu.make_async_copy(
             proj.at[window, tokens(me), :],
-            out_hbm.at[window, tokens(me), :],
+            field.at[window, tokens(me), :],
             out_own_sem.at[window],
         )
 
     loads = [
         pltpu.make_async_copy(source, target, load_sem.at[place])
         for place, (source, target) in enumerate(
-            ((qw_hbm, qw), (kw_hbm, kw), (vw_hbm, vw), (pw_hbm, pw))
+            (
+                (qw_hbm, qw),
+                (kw_hbm, kw),
+                (vw_hbm, vw),
+                (pw_hbm, pw),
+                (fk_hbm, fk),
+                (sk_hbm, sk),
+            )
         )
     ]
     for load in loads:
@@ -235,6 +259,8 @@
         lax.fori_loop(0, windows, step, 0)
 
     each_window(lambda window: own_q(window).start())
+    for halo in (halo_up, halo_down, side_right, side_left):
+        halo[...] = jnp.zeros_like(halo)
 
     barrier = pltpu.get_barrier_semaphore()
 
@@ -298,27 +324,218 @@
 
     each_window(across)
 
+    my_row, my_col = (lax.axis_index("row"), lax.axis_index("col"))
+    has_up, has_down = (my_row > 0, my_row < count_row - 1)
+    has_left, has_right = (my_col > 0, my_col < count_col - 1)
+    tokens_win = field.shape[1]
+    tile = TILE_COLS
+
+    def copy_to(source, target, sems, step_row, step_col):
+        return pltpu.make_async_remote_copy(
+            src_ref=source,
+            dst_ref=target,
+            send_sem=sems[0],
+            recv_sem=sems[1],
+            device_id={"row": my_row + step_row, "col": my_col + step_col},
+            device_id_type=pl.DeviceIdType.MESH,
+        )
+
+    def edge(window, down):
+        source = pl.ds(tokens_win - tile if down else 0, tile)
+        target = halo_up if down else halo_down
+        place = 0 if down else 1
+        return copy_to(
+            field.at[window, source, :],
+            target.at[window],
+            (edge_send.at[place, window], edge_recv.at[place, window]),
+            1 if down else -1,
+            0,
+        )
+
+    def side(right, step_row):
+        window = windows - 1 if right else 0
+        target = side_left if right else side_right
+        place = (0 if right else 3) + step_row + 1
+        if step_row == 0:
+            source, rows = (pl.ds(0, tokens_win), pl.ds(tile, tokens_win))
+        elif step_row > 0:
+            source, rows = (pl.ds(tokens_win - tile, tile), pl.ds(0, tile))
+        else:
+            source, rows = (pl.ds(0, tile), pl.ds(tokens_win + tile, tile))
+        return copy_to(
+            field.at[window, source, :],
+            target.at[rows, :],
+            (side_send.at[place], side_recv.at[place]),
+            step_row,
+            1 if right else -1,
+        )
+
+    row_ways = ((0, None, None), (1, has_down, has_up), (-1, has_up, has_down))
+
+    def send_sides(right):
+        there = has_right if right else has_left
+        for step_row, goes, _ in row_ways:
+
+            @pl.when(there if goes is None else there & goes)
+            def _():
+                side(right, step_row).start()
+
     def finish(window):
         own_r(window).wait()
         each_shift(lambda shift: copy_r(window, shift).wait())
-
-    each_window(finish)
-
-
-def attention_exchange(qw, kw, vw, qi, ki, proj_weight, proj_bias):
+        for down, goes in ((True, has_down), (False, has_up)):
+
+            @pl.when(goes)
+            def _():
+                edge(window, down).start()
+
+    finish(0)
+    send_sides(False)
+
+    def later(window, carry):
+        finish(window)
+        return carry
+
+    lax.fori_loop(1, windows, later, 0)
+    send_sides(True)
+
+    depth = fk.shape[-1]
+    width = (windows + 1) * tile
+    token_rows = tokens_win // tile
+    total = shuffled.shape[1]
+
+    for window in range(windows):
+        for line in range(token_rows):
+            start = tile + (line + 1) * width + window * tile
+            for parity in range(2):
+                shuffled[parity, start : start + tile, depth : 3 * depth] = field[
+                    window,
+                    line * tile : (line + 1) * tile,
+                    parity * 2 * depth : (parity + 1) * 2 * depth,
+                ]
+
+    for window in range(windows):
+        for down, goes, comes in ((True, has_down, has_up), (False, has_up, has_down)):
+
+            @pl.when(goes)
+            def _():
+                edge(window, down).wait_send()
+
+            @pl.when(comes)
+            def _():
+                edge(window, down).wait_recv()
+
+    for right in (True, False):
+        there, here = (has_right, has_left) if right else (has_left, has_right)
+        for step_row, goes, comes in row_ways:
+
+            @pl.when(there if goes is None else there & goes)
+            def _():
+                side(right, step_row).wait_send()
+
+            @pl.when(here if comes is None else here & comes)
+            def _():
+                side(right, step_row).wait_recv()
+
+    for parity in range(2):
+        lanes = slice(parity * 2 * depth, (parity + 1) * 2 * depth)
+        for window in range(windows):
+            for source, line in ((halo_up, 0), (halo_down, token_rows + 1)):
+                start = tile + line * width + window * tile
+                shuffled[parity, start : start + tile, depth : 3 * depth] = source[
+                    window, :, lanes
+                ]
+        first = lax.broadcasted_iota(jnp.int32, (tile, 2 * depth), 0) < tile // 2
+        shuffled[parity, 0:tile, depth : 3 * depth] = side_left[0:tile, lanes]
+        for line in range(token_rows + 2):
+            start = tile + line * width + windows * tile
+            block = side_right[line * tile : (line + 1) * tile, lanes]
+            if line < token_rows + 1:
+                after = side_left[(line + 1) * tile : (line + 2) * tile, lanes]
+                block = jnp.where(first, block, after)
+            shuffled[parity, start : start + tile, depth : 3 * depth] = block
+        odd = shuffled[parity, :, 2 * depth : 3 * depth].astype(jnp.float32)
+        shuffled[parity, :, 0:depth] = pltpu.roll(odd, 1, 0).astype(jnp.bfloat16)
+        even = shuffled[parity, :, depth : 2 * depth].astype(jnp.float32)
+        shuffled[parity, :, 3 * depth :] = pltpu.roll(even, total - 1, 0).astype(jnp.bfloat16)
+
+    def convolve_rows(source, weights, row_parity, col_parity, start, size):
+        if row_parity == 0:
+            taps = ((1, -width), (0, 0), (1, 0))
+        else:
+            taps = ((0, 0), (1, 0), (0, width))
+        result = None
+        for tap, (parity, shift) in enumerate(taps):
+            cells = source[
+                parity,
+                start + shift : start + shift + size,
+                col_parity * depth : (col_parity + 3) * depth,
+            ]
+            part = jnp.dot(cells, weights[tap], preferred_element_type=jnp.float32)
+            result = part if result is None else result + part
+        return result
+
+    size = total - width
+    main = windows * tile
+    right_stop = jnp.where(has_right, main + tile // 2, main)
+    left_start = jnp.where(has_left, main + tile // 2, width)
+    line_start = jnp.where(has_up, 0, 1)
+    line_stop = jnp.where(has_down, token_rows + 2, token_rows + 1)
+    for parity in range(2):
+        start = width if parity == 0 else 0
+        place = lax.broadcasted_iota(jnp.int32, (size, depth), 0) + start
+        column = lax.rem(place + (width - tile), width)
+        line = lax.div(place + (width - tile) + tile // 2, width) - 1
+        valid = (column < right_stop) | (column >= left_start)
+        valid = valid & ((line < line_stop) if parity == 0 else (line >= line_start))
+        for other in range(2):
+            value = convolve_rows(shuffled, fk, parity, other, start, size) + fb_ref[...]
+            value = jnp.where(valid, jax.nn.gelu(value), 0.0)
+            rows = slice(start, start + size)
+            activated[parity, rows, (other + 1) * depth : (other + 2) * depth] = value.astype(
+                jnp.bfloat16
+            )
+            if other == 1:
+                moved = pltpu.roll(value, 1, 0)
+                activated[parity, rows, 0:depth] = moved.astype(jnp.bfloat16)
+            else:
+                moved = pltpu.roll(value, size - 1, 0)
+                activated[parity, rows, 3 * depth :] = moved.astype(jnp.bfloat16)
+
+    for parity in range(2):
+        for other in range(2):
+            value = convolve_rows(
+                activated, sk, parity, other, tile + width, token_rows * width
+            )
+            value = (value + sb_ref[...]).astype(jnp.bfloat16)
+            for line in range(token_rows):
+                out_ref[2 * line + parity, :, other * depth : (other + 1) * depth] = value[
+                    line * width : line * width + windows * tile
+                ]
+
+
+def fused(qw, kw, vw, qi, ki, proj_weight, proj_bias, first_kernel, first_bias, second_kernel, second_bias):
     windows, tokens_win, features = qw.shape
     count_row = lax.axis_size("row")
     count_col = lax.axis_size("col")
     count = count_row * count_col
     owned = tokens_win // count
     channels = proj_weight.shape[-1]
+    depth = first_kernel.shape[-1]
+    taps = (first_kernel.shape[0], first_kernel.shape[1] * first_kernel.shape[2], depth)
+    token_rows = tokens_win // TILE_COLS
+    width = (windows + 1) * TILE_COLS
+    planes = (2, TILE_COLS + (token_rows + 2) * width, 4 * depth)
     whole = pl.BlockSpec(memory_space=pl.ANY)
+    held = pl.BlockSpec(memory_space=pltpu.VMEM)
     dma = pltpu.SemaphoreType.DMA
     return pl.pallas_call(
         functools.partial(attention_kernel, count_row, count_col),
-        out_shape=jax.ShapeDtypeStruct((windows, tokens_win, channels), jnp.bfloat16),
-        in_specs=[whole] * 6 + [pl.BlockSpec(memory_space=pltpu.VMEM)],
-        out_specs=whole,
+        out_shape=jax.ShapeDtypeStruct(
+            (2 * token_rows, windows * TILE_COLS, 2 * depth), jnp.bfloat16
+        ),
+        in_specs=[whole] * 8 + [held] * 3,
+        out_specs=held,
         scratch_shapes=[
             pltpu.VMEM(qw.shape, jnp.bfloat16),
             pltpu.VMEM(qw.shape, jnp.bfloat16),
@@ -329,7 +546,16 @@
             pltpu.VMEM((count, windows, owned, features), jnp.bfloat16),
             pltpu.VMEM((windows, count, owned, features), jnp.bfloat16),
             pltpu.VMEM((windows, tokens_win, channels), jnp.bfloat16),
-            dma((4,)),
+            pltpu.VMEM((windows, tokens_win, channels), jnp.bfloat16),
+            pltpu.VMEM(taps, jnp.bfloat16),
+            pltpu.VMEM(taps, jnp.bfloat16),
+            pltpu.VMEM((windows, TILE_COLS, channels), jnp.bfloat16),
+            pltpu.VMEM((windows, TILE_COLS, channels), jnp.bfloat16),
+            pltpu.VMEM((tokens_win + 2 * TILE_COLS, channels), jnp.bfloat16),
+            pltpu.VMEM((tokens_win + 2 * TILE_COLS, channels), jnp.bfloat16),
+            pltpu.VMEM(planes, jnp.bfloat16),
+            pltpu.VMEM(planes, jnp.bfloat16),
+            dma((6,)),
             dma((2,)),
             dma((windows,)),
             dma((windows,)),
@@ -341,11 +567,27 @@
             dma((windows, count)),
             dma((windows, count)),
             dma((windows, count)),
+            dma((2, windows)),
+            dma((2, windows)),
+            dma((6,)),
+            dma((6,)),
         ],
         compiler_params=pltpu.CompilerParams(
-            collective_id=0, has_side_effects=True, vmem_limit_bytes=48 * 1024 * 1024
+            collective_id=0, has_side_effects=True, vmem_limit_bytes=62 * 1024 * 1024
         ),
-    )(qw, kw, vw, qi, ki, proj_weight, proj_bias.reshape(1, channels))
+    )(
+        qw,
+        kw,
+        vw,
+        qi,
+        ki,
+        proj_weight,
+        first_kernel.reshape(taps),
+        second_kernel.reshape(taps),
+        proj_bias.reshape(1, channels),
+        first_bias.reshape(1, depth),
+        second_bias.reshape(1, depth),
+    )
 
 
 def convolutions(
@@ -375,8 +617,8 @@
     rows_dev, cols_dev, tokens_win, features = query_window.shape
     flat = (rows_dev * cols_dev, tokens_win, features)
     owners = lax.axis_size("row") * lax.axis_size("col")
-    if tokens_win % (owners * 8) == 0 and features % LANES == 0:
-        projected = attention_exchange(
+    if rows_dev == 1 and tokens_win % (owners * 8) == 0 and features % LANES == 0:
+        fine = fused(
             query_window.reshape(flat),
             key_window.reshape(flat),
             value_window.reshape(flat),
@@ -384,10 +626,12 @@
             key_index.reshape(flat),
             proj_weight,
             proj_bias,
-        )
-        return convolutions(
-            projected, rows_dev, cols_dev, first_kernel, first_bias, second_kernel, second_bias
-        )
+            first_kernel,
+            first_bias,
+            second_kernel,
+            second_bias,
+        )
+        return fine.reshape(fine.shape[0], 2 * fine.shape[1], -1)
     layout = (rows_dev * cols_dev, tokens_win, HEADS, HEAD_DIM)
     window_out = window_attend(
         query_window.reshape(layout), key_window.reshape(layout), value_window.reshape(layout)

time: 168 us -> 132 us (0.79)
  starting transfers between devices: 22.9 us -> 0 us
  Pallas kernels: 116 us -> 129 us
  matrix products: 9.54 us -> 0 us
  local copies, waits for them, and re-layouts: 8.97 us -> 2.2 us
  other arithmetic: 5.74 us -> 0 us
  waiting for transfers between devices: 4.94 us -> 0 us
    ppermute x8 -> x0, starting transfers between devices: 22.9 us -> none  [the longest x4 16.1 us: extended(): after = lax.ppermute(first, axis, down)]
    pallas_call x1, Pallas kernels: 116 us -> 129 us  [fused(): pl.pallas_call(functools.partial(attention_kernel, count_row, count_col),...]
    dot_general x18 -> x0, matrix products: 9.54 us -> none  [convolve(): jnp.dot(cells, kernel[row_shift, col_shift], preferred_element_type=jnp.f...]
    unnamed x17 -> x0, local copies, waits for them, and re-layouts: 5.11 us -> none
    concatenate x4 -> x0, other arithmetic: 5.04 us -> none  [extended(): value = jnp.concatenate([before, value, after], axis=dim)]
    ppermute x8 -> x0, waiting for transfers between devices: 4.94 us -> none  [the longest x4 3.8 us: extended(): before = lax.ppermute(last, axis, up)]
  transfers between devices with their start and end apart: 8 -> 0, of which waited for: 3 -> 0; matrix products, arithmetic and copies ran while one was open for 1% -> 0% of each run, Pallas kernels for 0% -> 0%
where the time goes in v2:
time: 132 us
  Pallas kernels  129 us (98%)
  local copies, waits for them, and re-layouts  2.2 us (2%)
    pallas_call x1, Pallas kernels, fused(): pl.pallas_call(functools.partial(attention_kernel, count_row, count_col),...  129 us

profile of v2, /device:TPU:17, one launch (start us, length us, event | category | flops | bytes accessed | tf_op | source)
XLA Modules:
  0.0 131.6 jit_solution(5588062291989631948)
XLA Ops:
  0.0 129.3 %shard_map.109 = bf16[16,64,512]{2,1,0:T(8,128)(2,1)} custom-call(bf16[4,128,1280]{2,1,0:T(8,128)(2,1)} %bitcast.10, bf16[4,128,1280]{2,1,0:T(8,128)(2,1)} %bitcast.11, bf16[4,128,1280]{2,1,0:T(8,128)(2,1)} %bitcast.12, bf16[4,128,1280]{2,1,0:T(8,128)(2,1)} %bitcast.13, bf16[4,128,1280]{2,1,0:T(8,128)(2,1)} %bitcast.14, bf16[1280,1024]{1,0:T(8,128)(2,1)} %pw_hbm.1, ...), custom_call_target="tpu_custom_call" | custom-call | tf_op jit(solution)/shard_map/pallas_call | solution.py:532
  129.4 2.2 %reshape.43 = bf16[16,128,256]{2,1,0:T(8,128)(2,1)} reshape(bf16[16,64,512]{2,1,0:T(8,128)(2,1)} %shard_map.109) | data formatting | bytes 2097152 | tf_op jit(solution)/shard_map/reshape | solution.py:634

commit v3 on v2

--- a/solution.py
+++ b/solution.py
@@ -157,6 +157,13 @@
     features = qw.shape[2]
     me = lax.axis_index("row") * count_col + lax.axis_index("col")
 
+    my_row, my_col = (lax.axis_index("row"), lax.axis_index("col"))
+    has_up, has_down = (my_row > 0, my_row < count_row - 1)
+    has_left, has_right = (my_col > 0, my_col < count_col - 1)
+
+    def ordered(step):
+        return jnp.where(has_left, step, windows - 1 - step)
+
     def offset(step):
         half = (step + 1) // 2
         return count // 2 + jnp.where(step % 2 == 1, half, -half)
@@ -195,7 +202,7 @@
     def copy_q(window, shift):
         peer = peer_of(shift)
         return pltpu.make_async_remote_copy(
-            src_ref=qi_hbm.at[window, tokens(peer), :],
+            src_ref=qi_hbm.at[ordered(window), tokens(peer), :],
             dst_ref=q_all.at[window, me],
             send_sem=q_send.at[window, shift],
             recv_sem=q_recv.at[window, shift],
@@ -216,7 +223,7 @@
 
     def own_q(window):
         return pltpu.make_async_copy(
-            qi_hbm.at[window, tokens(me), :], q_all.at[window, me], q_own_sem.at[window]
+            qi_hbm.at[ordered(window), tokens(me), :], q_all.at[window, me], q_own_sem.at[window]
         )
 
     def own_r(window):
@@ -261,6 +268,9 @@
     each_window(lambda window: own_q(window).start())
     for halo in (halo_up, halo_down, side_right, side_left):
         halo[...] = jnp.zeros_like(halo)
+    for outer in (0, windows + 1):
+        for parity in range(2):
+            activated[parity, outer] = jnp.zeros_like(activated[parity, outer])
 
     barrier = pltpu.get_barrier_semaphore()
 
@@ -324,9 +334,6 @@
 
     each_window(across)
 
-    my_row, my_col = (lax.axis_index("row"), lax.axis_index("col"))
-    has_up, has_down = (my_row > 0, my_row < count_row - 1)
-    has_left, has_right = (my_col > 0, my_col < count_col - 1)
     tokens_win = field.shape[1]
     tile = TILE_COLS
 
@@ -340,20 +347,19 @@
             device_id_type=pl.DeviceIdType.MESH,
         )
 
-    def edge(window, down):
+    def edge(step, down):
         source = pl.ds(tokens_win - tile if down else 0, tile)
         target = halo_up if down else halo_down
         place = 0 if down else 1
         return copy_to(
-            field.at[window, source, :],
-            target.at[window],
-            (edge_send.at[place, window], edge_recv.at[place, window]),
+            field.at[step, source, :],
+            target.at[step],
+            (edge_send.at[place, step], edge_recv.at[place, step]),
             1 if down else -1,
             0,
         )
 
     def side(right, step_row):
-        window = windows - 1 if right else 0
         target = side_left if right else side_right
         place = (0 if right else 3) + step_row + 1
         if step_row == 0:
@@ -363,7 +369,7 @@
         else:
             source, rows = (pl.ds(0, tile), pl.ds(tokens_win + tile, tile))
         return copy_to(
-            field.at[window, source, :],
+            field.at[0, source, :],
             target.at[rows, :],
             (side_send.at[place], side_recv.at[place]),
             step_row,
@@ -380,52 +386,7 @@
             def _():
                 side(right, step_row).start()
 
-    def finish(window):
-        own_r(window).wait()
-        each_shift(lambda shift: copy_r(window, shift).wait())
-        for down, goes in ((True, has_down), (False, has_up)):
-
-            @pl.when(goes)
-            def _():
-                edge(window, down).start()
-
-    finish(0)
-    send_sides(False)
-
-    def later(window, carry):
-        finish(window)
-        return carry
-
-    lax.fori_loop(1, windows, later, 0)
-    send_sides(True)
-
-    depth = fk.shape[-1]
-    width = (windows + 1) * tile
-    token_rows = tokens_win // tile
-    total = shuffled.shape[1]
-
-    for window in range(windows):
-        for line in range(token_rows):
-            start = tile + (line + 1) * width + window * tile
-            for parity in range(2):
-                shuffled[parity, start : start + tile, depth : 3 * depth] = field[
-                    window,
-                    line * tile : (line + 1) * tile,
-                    parity * 2 * depth : (parity + 1) * 2 * depth,
-                ]
-
-    for window in range(windows):
-        for down, goes, comes in ((True, has_down, has_up), (False, has_up, has_down)):
-
-            @pl.when(goes)
-            def _():
-                edge(window, down).wait_send()
-
-            @pl.when(comes)
-            def _():
-                edge(window, down).wait_recv()
-
-    for right in (True, False):
+    def wait_sides(right):
         there, here = (has_right, has_left) if right else (has_left, has_right)
         for step_row, goes, comes in row_ways:
 
@@ -437,81 +398,164 @@
             def _():
                 side(right, step_row).wait_recv()
 
-    for parity in range(2):
-        lanes = slice(parity * 2 * depth, (parity + 1) * 2 * depth)
-        for window in range(windows):
-            for source, line in ((halo_up, 0), (halo_down, token_rows + 1)):
-                start = tile + line * width + window * tile
-                shuffled[parity, start : start + tile, depth : 3 * depth] = source[
-                    window, :, lanes
+    def finish(step):
+        own_r(step).wait()
+        each_shift(lambda shift: copy_r(step, shift).wait())
+        for down, goes in ((True, has_down), (False, has_up)):
+
+            @pl.when(goes)
+            def _():
+                edge(step, down).start()
+
+    def wait_edges(step):
+        for down, goes, comes in ((True, has_down, has_up), (False, has_up, has_down)):
+
+            @pl.when(goes)
+            def _():
+                edge(step, down).wait_send()
+
+            @pl.when(comes)
+            def _():
+                edge(step, down).wait_recv()
+
+    depth = fk.shape[-1]
+    high = tokens_win + 2 * tile
+    size = high - tile
+    column = lax.rem(lax.broadcasted_iota(jnp.int32, (high, depth), 0), tile)
+
+    def lanes_of(parity):
+        return slice(parity * 2 * depth, (parity + 1) * 2 * depth)
+
+    def build(step):
+        place = ordered(step) + 1
+        for parity in range(2):
+            lanes = lanes_of(parity)
+            middle = slice(depth, 3 * depth)
+            shuffled[parity, place, 0:tile, middle] = halo_up[step, :, lanes]
+            shuffled[parity, place, tile : tile + tokens_win, middle] = field[step, :, lanes]
+            shuffled[parity, place, tile + tokens_win :, middle] = halo_down[step, :, lanes]
+
+    def shift_left(planes, parity, place):
+        near = planes[parity, place, :, 2 * depth : 3 * depth].astype(jnp.float32)
+        far = planes[parity, place - 1, :, 2 * depth : 3 * depth].astype(jnp.float32)
+        moved = jnp.where(
+            column == 0, pltpu.roll(far, high - (tile - 1), 0), pltpu.roll(near, 1, 0)
+        )
+        planes[parity, place, :, 0:depth] = moved.astype(jnp.bfloat16)
+
+    def shift_right(planes, parity, place):
+        near = planes[parity, place, :, depth : 2 * depth].astype(jnp.float32)
+        far = planes[parity, place + 1, :, depth : 2 * depth].astype(jnp.float32)
+        moved = jnp.where(
+            column == tile - 1, pltpu.roll(far, tile - 1, 0), pltpu.roll(near, high - 1, 0)
+        )
+        planes[parity, place, :, 3 * depth : 4 * depth] = moved.astype(jnp.bfloat16)
+
+    def shift(planes, steps):
+        for step in steps:
+            for parity in range(2):
+                shift_left(planes, parity, ordered(step) + 1)
+                shift_right(planes, parity, ordered(step) + 1)
+
+    def convolve_rows(source, weights, row_parity, col_parity, places, start, length):
+        if row_parity == 0:
+            taps = ((1, -tile), (0, 0), (1, 0))
+        else:
+            taps = ((0, 0), (1, 0), (0, tile))
+        result = None
+        for tap, (parity, move) in enumerate(taps):
+            cells = [
+                source[
+                    parity,
+                    place,
+                    start + move : start + move + length,
+                    col_parity * depth : (col_parity + 3) * depth,
                 ]
-        first = lax.broadcasted_iota(jnp.int32, (tile, 2 * depth), 0) < tile // 2
-        shuffled[parity, 0:tile, depth : 3 * depth] = side_left[0:tile, lanes]
-        for line in range(token_rows + 2):
-            start = tile + line * width + windows * tile
-            block = side_right[line * tile : (line + 1) * tile, lanes]
-            if line < token_rows + 1:
-                after = side_left[(line + 1) * tile : (line + 2) * tile, lanes]
-                block = jnp.where(first, block, after)
-            shuffled[parity, start : start + tile, depth : 3 * depth] = block
-        odd = shuffled[parity, :, 2 * depth : 3 * depth].astype(jnp.float32)
-        shuffled[parity, :, 0:depth] = pltpu.roll(odd, 1, 0).astype(jnp.bfloat16)
-        even = shuffled[parity, :, depth : 2 * depth].astype(jnp.float32)
-        shuffled[parity, :, 3 * depth :] = pltpu.roll(even, total - 1, 0).astype(jnp.bfloat16)
-
-    def convolve_rows(source, weights, row_parity, col_parity, start, size):
-        if row_parity == 0:
-            taps = ((1, -width), (0, 0), (1, 0))
-        else:
-            taps = ((0, 0), (1, 0), (0, width))
-        result = None
-        for tap, (parity, shift) in enumerate(taps):
-            cells = source[
-                parity,
-                start + shift : start + shift + size,
-                col_parity * depth : (col_parity + 3) * depth,
+                for place in places
             ]
+            cells = cells[0] if len(cells) == 1 else jnp.concatenate(cells, axis=0)
             part = jnp.dot(cells, weights[tap], preferred_element_type=jnp.float32)
             result = part if result is None else result + part
         return result
 
-    size = total - width
-    main = windows * tile
-    right_stop = jnp.where(has_right, main + tile // 2, main)
-    left_start = jnp.where(has_left, main + tile // 2, width)
-    line_start = jnp.where(has_up, 0, 1)
-    line_stop = jnp.where(has_down, token_rows + 2, token_rows + 1)
+    line = lax.broadcasted_iota(jnp.int32, (size, depth), 0)
+    line_stop = jnp.where(has_down, size, size - tile)
+    line_start = jnp.where(has_up, 0, tile)
+
+    def convolve_first(places, col_parities):
+        for parity in range(2):
+            start = tile if parity == 0 else 0
+            valid = (line < line_stop) if parity == 0 else (line >= line_start)
+            for other in col_parities:
+                value = convolve_rows(shuffled, fk, parity, other, places, start, size)
+                value = jax.nn.gelu(value + fb_ref[...])
+                for index, place in enumerate(places):
+                    kept = jnp.where(valid, value[index * size : (index + 1) * size], 0.0)
+                    activated[
+                        parity,
+                        place,
+                        start : start + size,
+                        (other + 1) * depth : (other + 2) * depth,
+                    ] = kept.astype(jnp.bfloat16)
+
+    def convolve_second(steps):
+        places = [ordered(step) + 1 for step in steps]
+        for parity in range(2):
+            for other in range(2):
+                value = convolve_rows(activated, sk, parity, other, places, tile, tokens_win)
+                value = (value + sb_ref[...]).astype(jnp.bfloat16)
+                for index, place in enumerate(places):
+                    begin = pl.multiple_of((place - 1) * tile, tile)
+                    for row in range(tokens_win // tile):
+                        at = index * tokens_win + row * tile
+                        out_ref[
+                            2 * row + parity,
+                            pl.ds(begin, tile),
+                            other * depth : (other + 1) * depth,
+                        ] = value[at : at + tile]
+
+    final = windows - 1
+    finish(0)
+    send_sides(False)
+    send_sides(True)
+    for step in range(1, final):
+        finish(step)
+    wait_sides(False)
+    wait_sides(True)
     for parity in range(2):
-        start = width if parity == 0 else 0
-        place = lax.broadcasted_iota(jnp.int32, (size, depth), 0) + start
-        column = lax.rem(place + (width - tile), width)
-        line = lax.div(place + (width - tile) + tile // 2, width) - 1
-        valid = (column < right_stop) | (column >= left_start)
-        valid = valid & ((line < line_stop) if parity == 0 else (line >= line_start))
-        for other in range(2):
-            value = convolve_rows(shuffled, fk, parity, other, start, size) + fb_ref[...]
-            value = jnp.where(valid, jax.nn.gelu(value), 0.0)
-            rows = slice(start, start + size)
-            activated[parity, rows, (other + 1) * depth : (other + 2) * depth] = value.astype(
-                jnp.bfloat16
-            )
-            if other == 1:
-                moved = pltpu.roll(value, 1, 0)
-                activated[parity, rows, 0:depth] = moved.astype(jnp.bfloat16)
-            else:
-                moved = pltpu.roll(value, size - 1, 0)
-                activated[parity, rows, 3 * depth :] = moved.astype(jnp.bfloat16)
-
-    for parity in range(2):
-        for other in range(2):
-            value = convolve_rows(
-                activated, sk, parity, other, tile + width, token_rows * width
-            )
-            value = (value + sb_ref[...]).astype(jnp.bfloat16)
-            for line in range(token_rows):
-                out_ref[2 * line + parity, :, other * depth : (other + 1) * depth] = value[
-                    line * width : line * width + windows * tile
-                ]
+        for place, source in ((0, side_left), (windows + 1, side_right)):
+            shuffled[parity, place, :, depth : 3 * depth] = source[:, lanes_of(parity)]
+    for step in range(final):
+        wait_edges(step)
+        build(step)
+
+    early = list(range(final - 1))
+    shift(shuffled, early)
+
+    @pl.when(has_left)
+    def _():
+        for parity in range(2):
+            shift_right(shuffled, parity, 0)
+        convolve_first([0], (1,))
+
+    @pl.when(has_right)
+    def _():
+        for parity in range(2):
+            shift_left(shuffled, parity, windows + 1)
+        convolve_first([windows + 1], (0,))
+
+    convolve_first([ordered(step) + 1 for step in early], (0, 1))
+    finish(final)
+    shift(activated, early[:-1])
+    convolve_second(early[:-1])
+    wait_edges(final)
+    build(final)
+    late = [final - 1, final]
+    shift(shuffled, late)
+    convolve_first([ordered(step) + 1 for step in late], (0, 1))
+    rest = early[-1:] + late
+    shift(activated, rest)
+    convolve_second(rest)
 
 
 def fused(qw, kw, vw, qi, ki, proj_weight, proj_bias, first_kernel, first_bias, second_kernel, second_bias):
@@ -524,8 +568,7 @@
     depth = first_kernel.shape[-1]
     taps = (first_kernel.shape[0], first_kernel.shape[1] * first_kernel.shape[2], depth)
     token_rows = tokens_win // TILE_COLS
-    width = (windows + 1) * TILE_COLS
-    planes = (2, TILE_COLS + (token_rows + 2) * width, 4 * depth)
+    planes = (2, windows + 2, tokens_win + 2 * TILE_COLS, 4 * depth)
     whole = pl.BlockSpec(memory_space=pl.ANY)
     held = pl.BlockSpec(memory_space=pltpu.VMEM)
     dma = pltpu.SemaphoreType.DMA
@@ -617,7 +660,8 @@
     rows_dev, cols_dev, tokens_win, features = query_window.shape
     flat = (rows_dev * cols_dev, tokens_win, features)
     owners = lax.axis_size("row") * lax.axis_size("col")
-    if rows_dev == 1 and tokens_win % (owners * 8) == 0 and features % LANES == 0:
+    small = rows_dev == 1 and cols_dev > 2 and lax.axis_size("col") == 2
+    if small and tokens_win % (owners * 8) == 0 and features % LANES == 0:
         fine = fused(
             query_window.reshape(flat),
             key_window.reshape(flat),

time: 132 us -> 133 us (level)
  no operation moved by 1% of the time
where the time goes in v3:
time: 133 us; the launch traced here: 132 us
  Pallas kernels  130 us (98%)
  local copies, waits for them, and re-layouts  2.2 us (2%)
    pallas_call x1, Pallas kernels, fused(): pl.pallas_call(functools.partial(attention_kernel, count_row, count_col),...  130 us

profile of v3, /device:TPU:17, one launch (start us, length us, event | category | flops | bytes accessed | tf_op | source)
XLA Modules:
  0.0 131.7 jit_solution(7313372942214660942)
XLA Ops:
  0.0 129.5 %shard_map.109 = bf16[16,64,512]{2,1,0:T(8,128)(2,1)} custom-call(bf16[4,128,1280]{2,1,0:T(8,128)(2,1)} %bitcast.10, bf16[4,128,1280]{2,1,0:T(8,128)(2,1)} %bitcast.11, bf16[4,128,1280]{2,1,0:T(8,128)(2,1)} %bitcast.12, bf16[4,128,1280]{2,1,0:T(8,128)(2,1)} %bitcast.13, bf16[4,128,1280]{2,1,0:T(8,128)(2,1)} %bitcast.14, bf16[1280,1024]{1,0:T(8,128)(2,1)} %pw_hbm.1, ...), custom_call_target="tpu_custom_call" | custom-call | tf_op jit(solution)/shard_map/pallas_call | solution.py:575
  129.5 2.2 %reshape.43 = bf16[16,128,256]{2,1,0:T(8,128)(2,1)} reshape(bf16[16,64,512]{2,1,0:T(8,128)(2,1)} %shard_map.109) | data formatting | bytes 2097152 | tf_op jit(solution)/shard_map/reshape | solution.py:678

commit v4 on v2

--- a/solution.py
+++ b/solution.py
@@ -276,6 +276,15 @@
     pl.semaphore_wait(barrier, count - 1)
     each_shift(lambda shift: copy_k(shift).start())
 
+    def send_q(first, stop):
+        def step(window, carry):
+            each_shift(lambda shift: copy_q(window, shift).start())
+            return carry
+
+        lax.fori_loop(first, stop, step, 0)
+
+    send_q(0, windows // 2)
+
     for load in loads:
         load.wait()
 
@@ -293,7 +302,7 @@
     )
     own_v.start()
     each_shift(lambda shift: copy_v(shift).start())
-    each_window(lambda window: each_shift(lambda shift: copy_q(window, shift).start()))
+    send_q(windows // 2, windows)
 
     own_k.wait()
     own_v.wait()

time: 132 us -> 132 us (level)
  no operation moved by 1% of the time
where the time goes in v4:
time: 132 us
  Pallas kernels  129 us (98%)
  local copies, waits for them, and re-layouts  2.2 us (2%)
    pallas_call x1, Pallas kernels, fused(): pl.pallas_call(functools.partial(attention_kernel, count_row, count_col),...  129 us

profile of v4, /device:TPU:17, one launch (start us, length us, event | category | flops | bytes accessed | tf_op | source)
XLA Modules:
  0.0 131.6 jit_solution(9775187007206199336)
XLA Ops:
  0.0 129.3 %shard_map.109 = bf16[16,64,512]{2,1,0:T(8,128)(2,1)} custom-call(bf16[4,128,1280]{2,1,0:T(8,128)(2,1)} %bitcast.10, bf16[4,128,1280]{2,1,0:T(8,128)(2,1)} %bitcast.11, bf16[4,128,1280]{2,1,0:T(8,128)(2,1)} %bitcast.12, bf16[4,128,1280]{2,1,0:T(8,128)(2,1)} %bitcast.13, bf16[4,128,1280]{2,1,0:T(8,128)(2,1)} %bitcast.14, bf16[1280,1024]{1,0:T(8,128)(2,1)} %pw_hbm.1, ...), custom_call_target="tpu_custom_call" | custom-call | tf_op jit(solution)/shard_map/pallas_call | solution.py:541
  129.4 2.2 %reshape.43 = bf16[16,128,256]{2,1,0:T(8,128)(2,1)} reshape(bf16[16,64,512]{2,1,0:T(8,128)(2,1)} %shard_map.109) | data formatting | bytes 2097152 | tf_op jit(solution)/shard_map/reshape | solution.py:643
